TPU v7x, 512 devices: a whole 4x8x8 slice. The times are simulated.
512 devices in a mesh: row: 16 (over y_hi, x), col: 32 (over z, y_lo, core).
Axes of the slice: x: 4, y: 8 (y_hi: 4, y_lo: 2; y = y_hi * 2 + y_lo), z: 8, core: 2. Of those that a mesh axis runs over, the one named last changes fastest.
Arguments:
- query: bfloat16 [16384, 1024], P(('row', 'col')), may hold values from -0.5375 to 0.5375
- passage: bfloat16 [16384, 1024], P(('row', 'col')), may hold values from -0.43 to 0.43
- positive: int32 [512, 32], P(('row', 'col')), may hold values from 0 to 31, each once within a row
Outputs:
- loss_value: float32 [], replicated
- grad_query: bfloat16 [16384, 1024], P(('row', 'col'))
- grad_passage: bfloat16 [16384, 1024], P(('row', 'col'))
Inputs may be any that keep to these rules, and one draw needn't show every extreme that they name: Each row of positive names every position 0 to 31 once.
All inputs are finite; a program needn't handle non-finite values.
Results may differ from a plain program's by a relative error of at most 0.015.
Values may be sent and summed in bfloat16 or wider, within the bound.
No kernel may reach another device: no remote copies, remote signals or barrier semaphores. Data moves between devices by JAX's collectives and lax.ppermute only.
A program may use at most 64 MiB of HBM per device.

v0:
```python
import jax
import jax.numpy as jnp
from jax import lax
from jax.sharding import Mesh, PartitionSpec as P


logit_scale = 20.0

AXES = ("yh", "x", "z", "yl", "core")
SIZES = (4, 4, 8, 2, 2)
PASS_AXES = ("x", "yh")
CHIP_AXES = ("z", "yl")
LANES = 128


def exchange(blocks, axes):
    return lax.all_to_all(blocks, axes, 0, 0, tiled=True)


def spread(x, n):
    return lax.optimization_barrier(jnp.broadcast_to(x[None], (n,) + x.shape))


def swap_core(x):
    return lax.ppermute(x, "core", [(0, 1), (1, 0)])


def shift_x(x, d):
    n = lax.axis_size("x")
    return lax.ppermute(x, "x", [(i, (i + d) % n) for i in range(n)])


def scores_of(q, p):
    return logit_scale * lax.dot_general(
        q, p, (((1,), (1,)), ((), ())), preferred_element_type=jnp.float32
    )


def lse(x, axis):
    peak = x.max(axis=axis)
    return peak + jnp.log(jnp.exp(x - jnp.expand_dims(peak, axis)).sum(axis=axis))


def lse2(a, b):
    peak = jnp.maximum(a, b)
    return peak + jnp.log(jnp.exp(a - peak) + jnp.exp(b - peak))


def lanes_of(x, rows):
    hi = lax.reduce_precision(x, 8, 7)
    mid = lax.reduce_precision(x - hi, 8, 7)
    low = x - hi - mid
    lane = lax.broadcasted_iota(jnp.int32, (rows, LANES), 1)
    zero = jnp.zeros((rows, LANES), jnp.float32)
    return jnp.where(lane == 0, hi, jnp.where(lane == 1, mid, jnp.where(lane == 2, low, zero)))


def inner(query, passage, positive):
    rows, embed = query.shape
    n_pass = lax.axis_size(PASS_AXES)
    n_x = lax.axis_size("x")
    n_yh = lax.axis_size("yh")
    n_chip = lax.axis_size(CHIP_AXES)
    n_p = n_pass * rows
    half = n_chip * rows
    x_at = lax.axis_index("x")

    near = exchange(spread(passage, n_yh), "yh").reshape(n_yh * rows, embed)
    own = exchange(spread(query, n_chip), CHIP_AXES).reshape(half, embed)
    far = [shift_x(near, n_x - d) for d in range(1, n_x)]
    pall = lax.optimization_barrier(jnp.concatenate([near] + far, axis=0))
    other = swap_core(own)

    slot = jnp.arange(rows, dtype=jnp.int32)
    onehot = (positive[0][:, None] == slot[None, :]).astype(jnp.bfloat16)
    paired_passage = jnp.dot(onehot, passage, preferred_element_type=jnp.float32)
    paired_query = lax.dot_general(
        onehot, query, (((0,), (0,)), ((), ())), preferred_element_type=jnp.float32
    )
    positive_sum = logit_scale * jnp.sum(query.astype(jnp.float32) * paired_passage)

    s0 = scores_of(own, pall)
    s1 = scores_of(other, pall)
    row0, row1 = lse(s0, 1), lse(s1, 1)
    rows_mine = jnp.concatenate([row0.reshape(-1, LANES), row1.reshape(-1, LANES)], axis=0)
    rows_theirs = swap_core(rows_mine)
    col_peak = jnp.maximum(s0.max(axis=0), s1.max(axis=0))
    col_part = col_peak + jnp.log(
        jnp.exp(s0 - col_peak[None, :]).sum(axis=0) + jnp.exp(s1 - col_peak[None, :]).sum(axis=0)
    )

    place = jnp.arange(n_x, dtype=jnp.int32)
    moved = ((place[:, None] - x_at + n_x) % n_x == place[None, :])[:, :, None]
    col_part = jnp.where(moved, col_part.reshape(1, n_x, n_yh * rows), 0.0).sum(axis=1)
    col_all = exchange(spread(col_part.reshape(-1, LANES), n_pass), PASS_AXES)
    col_lse = lse(col_all, 0).reshape(n_x, 1, n_yh * rows)
    col_lse = jnp.where(moved, col_lse, 0.0).sum(axis=0).reshape(n_p)

    k = half // LANES
    pair = lse2(rows_mine, jnp.concatenate([rows_theirs[k:], rows_theirs[:k]], axis=0))
    lane = lax.broadcasted_iota(jnp.int32, (8, LANES), 1)
    extra = jnp.where(lane == 0, jnp.sum(col_lse), jnp.where(lane == 1, positive_sum, 0.0))
    row_all = exchange(spread(jnp.concatenate([pair, extra], axis=0), n_chip), CHIP_AXES)
    row_lse = lse(row_all[:, : 2 * k], 0)
    row_lse0, row_lse1 = row_lse[:k].reshape(half), row_lse[k:].reshape(half)
    totals = row_all[:, 2 * k].sum(axis=0)
    part = 0.5 * jnp.sum(row_lse) + totals[0] / n_pass - 2.0 * totals[1]

    def weights(s, row_lse):
        return (0.5 * (jnp.exp(s - row_lse[:, None]) + jnp.exp(s - col_lse[None, :]))).astype(
            jnp.bfloat16
        )

    w1 = weights(s1, row_lse1)
    w0 = weights(s0, row_lse0)
    given = jnp.dot(w1, pall, preferred_element_type=jnp.float32).astype(jnp.bfloat16)
    taken = swap_core(given)
    qgrad = jnp.dot(w0, pall, preferred_element_type=jnp.float32) + taken.astype(jnp.float32)
    qgrad = exchange(qgrad.astype(jnp.bfloat16).reshape(n_chip, rows, embed), CHIP_AXES)

    tn = (((0,), (0,)), ((), ()))
    pgrad = lax.dot_general(w0, own, tn, preferred_element_type=jnp.float32) + lax.dot_general(
        w1, other, tn, preferred_element_type=jnp.float32
    )
    pgrad = pgrad.reshape(n_x, n_yh * rows, embed)

    def with_lanes(block, value):
        return jnp.concatenate([block, lanes_of(value, block.shape[0])], axis=1).astype(
            jnp.bfloat16
        )

    got = [shift_x(with_lanes(pgrad[d], part), d) for d in range(1, n_x)]
    mid = pgrad[0] + sum(g[:, :embed].astype(jnp.float32) for g in got)
    part = part + sum(g[0, embed:].astype(jnp.float32).sum() for g in got)
    part = part + swap_core(jnp.broadcast_to(part, (8, LANES)))[0, 0]
    mid = exchange(with_lanes(mid, part).reshape(n_yh, rows, embed + LANES), "yh")
    passage_sum = mid[:, :, :embed].astype(jnp.float32).sum(axis=0)
    part = mid[:, 0, embed:].astype(jnp.float32).sum()
    loss = part / (2.0 * n_pass * n_chip * 2 * rows)

    query_sum = qgrad.astype(jnp.float32).sum(axis=0)
    grad_query = (logit_scale * (query_sum - paired_passage)).astype(jnp.bfloat16)
    grad_passage = (logit_scale * (passage_sum - paired_query)).astype(jnp.bfloat16)
    return (loss, grad_query, grad_passage)


def solution(mesh):
    cut = Mesh(mesh.devices.reshape(SIZES), AXES)
    spec = P(AXES, None)
    return jax.shard_map(
        inner,
        mesh=cut,
        in_specs=(spec, spec, spec),
        out_specs=(P(), spec, spec),
        check_vma=False,
    )
```

profile of v0, /device:TPU:1, one launch (start us, length us, event | category | flops | bytes accessed | tf_op | source)
XLA Modules:
  0.0 200.2 jit_solution(13892548418954569338)
XLA Ops:
  0.7 2.0 broadcast_in_dim.111
  2.7 12.0 %all-to-all-start.1 = ((bf16[16,32,1024]{2,1,0:T(8,128)(2,1)}), bf16[16,32,1024]{2,1,0:T(8,128)(2,1)S(1)}, u32[]{:S(2)}, u32[]{:S(2)}) async-start(bf16[16,32,1024]{2,1,0:T(8,128)(2,1)} %broadcast_in_dim.111), calls=%async_computation.1 | async-start | bytes 2097152 | tf_op jit(solution)/shard_map/all_to_all | solution.py:17
  14.6 0.7 broadcast_in_dim.110
  15.4 25.6 %all-to-all-done.1 = bf16[16,32,1024]{2,1,0:T(8,128)(2,1)S(1)} async-done(((bf16[16,32,1024]{2,1,0:T(8,128)(2,1)}), bf16[16,32,1024]{2,1,0:T(8,128)(2,1)S(1)}, u32[]{:S(2)}, u32[]{:S(2)}) %all-to-all-start.1) | async-done | bytes 1048608 | tf_op jit(solution)/shard_map/all_to_all | solution.py:17
  41.0 5.9 %all-to-all-start = ((bf16[4,32,1024]{2,1,0:T(8,128)(2,1)}), bf16[4,32,1024]{2,1,0:T(8,128)(2,1)S(1)}, u32[]{:S(2)}, u32[]{:S(2)}) async-start(bf16[4,32,1024]{2,1,0:T(8,128)(2,1)} %broadcast_in_dim.110), calls=%async_computation | async-start | bytes 524288 | tf_op jit(solution)/shard_map/all_to_all | solution.py:17
  46.9 4.4 %collective-permute-start.3 = (bf16[512,1024]{1,0:T(8,128)(2,1)S(1)}, bf16[512,1024]{1,0:T(8,128)(2,1)S(1)}, u32[]{:S(2)}, u32[]{:S(2)}) collective-permute-start(bf16[512,1024]{1,0:T(8,128)(2,1)S(1)} %bitcast.30), channel_id=1, source_target_pairs={{0,1},{1,0},{2,3},{3,2},{4,5},{5,4},{6,7},{7,6},{8,9},{9,8},{10,11... | collective-permute-start | bytes 3145736 | tf_op jit(solution)/shard_map/ppermute | solution.py:25
  51.4 1.5 multiply_reduce_fusion
  53.5 1.5 all-to-all-done
  55.0 3.1 %collective-permute-start.2 = (bf16[128,1024]{1,0:T(8,128)(2,1)S(1)}, bf16[128,1024]{1,0:T(8,128)(2,1)S(1)}, u32[]{:S(2)}, u32[]{:S(2)}) collective-permute-start(bf16[128,1024]{1,0:T(8,128)(2,1)S(1)} %bitcast.34), channel_id=1, source_target_pairs={{0,32},{32,64},{64,96},{96,0},{1,33},{33,65},{65,97},{97,1},{2,34}... | collective-permute-start | bytes 786440 | tf_op jit(solution)/shard_map/ppermute | solution.py:30
  58.1 4.4 %collective-permute-start.1 = (bf16[128,1024]{1,0:T(8,128)(2,1)S(1)}, bf16[128,1024]{1,0:T(8,128)(2,1)S(1)}, u32[]{:S(2)}, u32[]{:S(2)}) collective-permute-start(bf16[128,1024]{1,0:T(8,128)(2,1)S(1)} %bitcast.35), channel_id=1, source_target_pairs={{0,64},{32,96},{64,0},{96,32},{1,65},{33,97},{65,1},{97,33},{2,66}... | collective-permute-start | bytes 786440 | tf_op jit(solution)/shard_map/ppermute | solution.py:30
  62.5 3.1 %collective-permute-start = (bf16[128,1024]{1,0:T(8,128)(2,1)S(1)}, bf16[128,1024]{1,0:T(8,128)(2,1)S(1)}, u32[]{:S(2)}, u32[]{:S(2)}) collective-permute-start(bf16[128,1024]{1,0:T(8,128)(2,1)S(1)} %bitcast.36), channel_id=1, source_target_pairs={{0,96},{32,0},{64,32},{96,64},{1,97},{33,1},{65,33},{97,65},{2,98}... | collective-permute-start | bytes 786440 | tf_op jit(solution)/shard_map/ppermute | solution.py:30
  65.7 2.5 %collective-permute-done.1 = bf16[128,1024]{1,0:T(8,128)(2,1)S(1)} collective-permute-done((bf16[128,1024]{1,0:T(8,128)(2,1)S(1)}, bf16[128,1024]{1,0:T(8,128)(2,1)S(1)}, u32[]{:S(2)}, u32[]{:S(2)}) %collective-permute-start.1) | collective-permute-done | bytes 262176 | tf_op jit(solution)/shard_map/ppermute | solution.py:30
  68.1 3.3 %collective-permute-done = bf16[128,1024]{1,0:T(8,128)(2,1)S(1)} collective-permute-done((bf16[128,1024]{1,0:T(8,128)(2,1)S(1)}, bf16[128,1024]{1,0:T(8,128)(2,1)S(1)}, u32[]{:S(2)}, u32[]{:S(2)}) %collective-permute-start) | collective-permute-done | bytes 262176 | tf_op jit(solution)/shard_map/ppermute | solution.py:30
  71.5 0.8 fusion.13
  72.3 0.8 fusion.14
  73.2 0.7 exponential_reduce_fusion.2
  73.9 6.4 %collective-permute-start.4 = (f32[8,128]{1,0:T(8,128)S(1)}, f32[8,128]{1,0:T(8,128)S(1)}, u32[]{:S(2)}, u32[]{:S(2)}) collective-permute-start(f32[8,128]{1,0:T(8,128)S(1)} %pad_maximum_fusion.6), channel_id=1, source_target_pairs={{0,1},{1,0},{2,3},{3,2},{4,5},{5,4},{6,7},{7,6},{8,9},{9,8},{10,11... | collective-permute-start | bytes 12296 | tf_op jit(solution)/shard_map/ppermute | solution.py:25
  80.5 0.6 broadcast_in_dim.115
  81.1 7.1 %all-to-all-start.2 = ((f32[16,4,128]{2,1,0:T(4,128)}), f32[16,4,128]{2,1,0:T(4,128)S(1)}, u32[]{:S(2)}, u32[]{:S(2)}) async-start(f32[16,4,128]{2,1,0:T(4,128)} %broadcast_in_dim.115), calls=%async_computation.2 | async-start | bytes 65536 | tf_op jit(solution)/shard_map/all_to_all | solution.py:17
  88.2 8.8 %all-to-all-done.2 = f32[16,4,128]{2,1,0:T(4,128)S(1)} async-done(((f32[16,4,128]{2,1,0:T(4,128)}), f32[16,4,128]{2,1,0:T(4,128)S(1)}, u32[]{:S(2)}, u32[]{:S(2)}) %all-to-all-start.2) | async-done | bytes 32800 | tf_op jit(solution)/shard_map/all_to_all | solution.py:17
  97.1 0.7 select_reduce_fusion
  97.8 0.6 broadcast_select_fusion
  98.5 0.7 broadcast_in_dim.120
  99.1 4.4 %all-to-all-start.3 = ((f32[16,16,128]{2,1,0:T(8,128)}), f32[16,16,128]{2,1,0:T(8,128)S(1)}, u32[]{:S(2)}, u32[]{:S(2)}) async-start(f32[16,16,128]{2,1,0:T(8,128)} %broadcast_in_dim.120), calls=%async_computation.3 | async-start | bytes 262144 | tf_op jit(solution)/shard_map/all_to_all | solution.py:17
  103.5 8.0 %all-to-all-done.3 = f32[16,16,128]{2,1,0:T(8,128)S(1)} async-done(((f32[16,16,128]{2,1,0:T(8,128)}), f32[16,16,128]{2,1,0:T(8,128)S(1)}, u32[]{:S(2)}, u32[]{:S(2)}) %all-to-all-start.3) | async-done | bytes 131104 | tf_op jit(solution)/shard_map/all_to_all | solution.py:17
  111.6 0.6 fusion.15
  117.2 2.2 %fusion.12 = f32[512,1024]{1,0:T(8,128)S(1)} fusion(bf16[512,1024]{1,0:T(8,128)(2,1)} %bitcast.32, f32[512,512]{1,0:T(8,128)S(1)} %get-tuple-element.31, f32[512]{0:T(512)S(1)} %bitcast.39, f32[512]{0:T(512)S(1)} %get-tuple-element.22), kind=kOutput, calls=%fused_computation.69 | convolution fusion | flops 538181632 | bytes 4198400 | tf_op jit(solution)/shard_map/dot_general | solution.py:122
  119.4 0.9 fusion.19
  120.3 1.4 select_convert_fusion.1
  121.7 0.8 pad_maximum_fusion.1
  122.5 2.2 %collective-permute-start.5 = (bf16[128,1152]{1,0:T(8,128)(2,1)S(1)}, bf16[128,1152]{1,0:T(8,128)(2,1)S(1)}, u32[]{:S(2)}, u32[]{:S(2)}) collective-permute-start(bf16[128,1152]{1,0:T(8,128)(2,1)S(1)} %get-tuple-element.20), channel_id=1, source_target_pairs={{0,32},{32,64},{64,96},{96,0},{1,33},{33,65},{65,97},{97,1},{2,34}... | collective-permute-start | bytes 884744 | tf_op jit(solution)/shard_map/ppermute | solution.py:30
  124.6 3.7 %collective-permute-start.6 = (bf16[128,1152]{1,0:T(8,128)(2,1)S(1)}, bf16[128,1152]{1,0:T(8,128)(2,1)S(1)}, u32[]{:S(2)}, u32[]{:S(2)}) collective-permute-start(bf16[128,1152]{1,0:T(8,128)(2,1)S(1)} %get-tuple-element.19), channel_id=1, source_target_pairs={{0,64},{32,96},{64,0},{96,32},{1,65},{33,97},{65,1},{97,33},{2,66}... | collective-permute-start | bytes 884744 | tf_op jit(solution)/shard_map/ppermute | solution.py:30
  128.3 3.2 %collective-permute-start.7 = (bf16[128,1152]{1,0:T(8,128)(2,1)}, bf16[128,1152]{1,0:T(8,128)(2,1)S(1)}, u32[]{:S(2)}, u32[]{:S(2)}) collective-permute-start(bf16[128,1152]{1,0:T(8,128)(2,1)} %get-tuple-element.18), channel_id=1, source_target_pairs={{0,96},{32,0},{64,32},{96,64},{1,97},{33,1},{65,33},{97,65},{2,98}... | collective-permute-start | bytes 884744 | tf_op jit(solution)/shard_map/ppermute | solution.py:30
  131.5 1.9 convolution_convert_fusion
  133.4 5.3 %collective-permute-start.9 = (bf16[512,1024]{1,0:T(8,128)(2,1)}, bf16[512,1024]{1,0:T(8,128)(2,1)}, u32[]{:S(2)}, u32[]{:S(2)}) collective-permute-start(bf16[512,1024]{1,0:T(8,128)(2,1)} %convolution_convert_fusion), channel_id=1, source_target_pairs={{0,1},{1,0},{2,3},{3,2},{4,5},{5,4},{6,7},{7,6},{8,9},{9,8},{10,11... | collective-permute-start | bytes 3145736 | tf_op jit(solution)/shard_map/ppermute | solution.py:25
  139.5 0.7 copy-done.11
  142.1 0.6 fusion.9
  143.4 4.5 %collective-permute-start.8 = (f32[8,128]{1,0:T(8,128)S(1)}, f32[8,128]{1,0:T(8,128)S(1)}, u32[]{:S(2)}, u32[]{:S(2)}) collective-permute-start(f32[8,128]{1,0:T(8,128)S(1)} %broadcast_in_dim.124), channel_id=1, source_target_pairs={{0,1},{1,0},{2,3},{3,2},{4,5},{5,4},{6,7},{7,6},{8,9},{9,8},{10,11... | collective-permute-start | bytes 12296 | tf_op jit(solution)/shard_map/ppermute | solution.py:25
  147.9 1.2 fusion.2
  152.6 1.3 select_convert_fusion
  153.9 0.7 pad_maximum_fusion.4
  154.7 3.5 %all-to-all-start.4 = ((bf16[4,32,1152]{2,1,0:T(8,128)(2,1)}), bf16[4,32,1152]{2,1,0:T(8,128)(2,1)S(1)}, u32[]{:S(2)}, u32[]{:S(2)}) async-start(bf16[4,32,1152]{2,1,0:T(8,128)(2,1)} %pad_maximum_fusion.4), calls=%async_computation.4 | async-start | bytes 589824 | tf_op jit(solution)/shard_map/all_to_all | solution.py:17
  158.1 3.5 %add_convert_fusion = bf16[512,1024]{1,0:T(8,128)(2,1)} fusion(bf16[512,1024]{1,0:T(8,128)(2,1)} %collective-permute-done.9, bf16[512,1024]{1,0:T(8,128)(2,1)} %copy-done.4, f32[512,512]{1,0:T(8,128)S(1)} %copy-done.3, f32[512]{0:T(512)S(1)} %bitcast.42, f32[512]{0:T(512)S(1)} %get-tuple-element.22), kind=kOutput, calls=%fused_computation.1 | convolution fusion | flops 539754496 | bytes 4198400 | tf_op jit(solution)/shard_map/dot_general | solution.py:118
  161.6 6.9 %all-to-all-done.4 = bf16[4,32,1152]{2,1,0:T(8,128)(2,1)S(1)} async-done(((bf16[4,32,1152]{2,1,0:T(8,128)(2,1)}), bf16[4,32,1152]{2,1,0:T(8,128)(2,1)S(1)}, u32[]{:S(2)}, u32[]{:S(2)}) %all-to-all-start.4) | async-done | bytes 294944 | tf_op jit(solution)/shard_map/all_to_all | solution.py:17
  168.5 3.7 %all-to-all-start.5 = ((bf16[16,32,1024]{2,1,0:T(8,128)(2,1)}), bf16[16,32,1024]{2,1,0:T(8,128)(2,1)S(1)}, u32[]{:S(2)}, u32[]{:S(2)}) async-start(bf16[16,32,1024]{2,1,0:T(8,128)(2,1)} %bitcast.14), calls=%async_computation.5 | async-start | bytes 2097152 | tf_op jit(solution)/shard_map/all_to_all | solution.py:17
  173.4 0.9 fusion.1
  174.3 23.8 %all-to-all-done.5 = bf16[16,32,1024]{2,1,0:T(8,128)(2,1)S(1)} async-done(((bf16[16,32,1024]{2,1,0:T(8,128)(2,1)}), bf16[16,32,1024]{2,1,0:T(8,128)(2,1)S(1)}, u32[]{:S(2)}, u32[]{:S(2)}) %all-to-all-start.5) | async-done | bytes 1048608 | tf_op jit(solution)/shard_map/all_to_all | solution.py:17
  198.4 0.6 multiply_convert_fusion.2
  (68 shorter events, 3.8 us)
Async XLA Ops:
  0.6 50.7 %copy-start.7 = (bf16[32,1024]{1,0:T(8,128)(2,1)S(1)}, bf16[32,1024]{1,0:T(8,128)(2,1)}, u32[]{:S(2)}) copy-start(bf16[32,1024]{1,0:T(8,128)(2,1)} %param.3) | copy-start | bytes 196612
  0.6 14.0 %copy-start.9 = (bf16[32,1024]{1,0:T(8,128)(2,1)S(1)}, bf16[32,1024]{1,0:T(8,128)(2,1)}, u32[]{:S(2)}) copy-start(bf16[32,1024]{1,0:T(8,128)(2,1)} %param.4) | copy-start | bytes 196612
  0.7 50.7 %copy-start.13 = (s32[1,32]{1,0:T(1,128)S(1)}, s32[1,32]{1,0:T(1,128)}, u32[]{:S(2)}) copy-start(s32[1,32]{1,0:T(1,128)} %param.5) | copy-start | bytes 388
  2.7 38.4 %all-to-all-start.1 = ((bf16[16,32,1024]{2,1,0:T(8,128)(2,1)}), bf16[16,32,1024]{2,1,0:T(8,128)(2,1)S(1)}, u32[]{:S(2)}, u32[]{:S(2)}) async-start(bf16[16,32,1024]{2,1,0:T(8,128)(2,1)} %broadcast_in_dim.111), calls=%async_computation.1 | async-start | bytes 2097152 | tf_op jit(solution)/shard_map/all_to_all | solution.py:17
  41.0 31.3 %copy-start.6 = (bf16[16,32,1024]{2,1,0:T(8,128)(2,1)}, bf16[16,32,1024]{2,1,0:T(8,128)(2,1)S(1)}, u32[]{:S(2)}) copy-start(bf16[16,32,1024]{2,1,0:T(8,128)(2,1)S(1)} %all-to-all-done.1) | copy-start | bytes 3145732
  41.0 14.0 %all-to-all-start = ((bf16[4,32,1024]{2,1,0:T(8,128)(2,1)}), bf16[4,32,1024]{2,1,0:T(8,128)(2,1)S(1)}, u32[]{:S(2)}, u32[]{:S(2)}) async-start(bf16[4,32,1024]{2,1,0:T(8,128)(2,1)} %broadcast_in_dim.110), calls=%async_computation | async-start | bytes 524288 | tf_op jit(solution)/shard_map/all_to_all | solution.py:17
  46.9 25.4 %collective-permute-start.3 = (bf16[512,1024]{1,0:T(8,128)(2,1)S(1)}, bf16[512,1024]{1,0:T(8,128)(2,1)S(1)}, u32[]{:S(2)}, u32[]{:S(2)}) collective-permute-start(bf16[512,1024]{1,0:T(8,128)(2,1)S(1)} %bitcast.30), channel_id=1, source_target_pairs={{0,1},{1,0},{2,3},{3,2},{4,5},{5,4},{6,7},{7,6},{8,9},{9,8},{10,11... | collective-permute-start | bytes 3145736 | tf_op jit(solution)/shard_map/ppermute | solution.py:25
  55.0 10.6 %collective-permute-start.2 = (bf16[128,1024]{1,0:T(8,128)(2,1)S(1)}, bf16[128,1024]{1,0:T(8,128)(2,1)S(1)}, u32[]{:S(2)}, u32[]{:S(2)}) collective-permute-start(bf16[128,1024]{1,0:T(8,128)(2,1)S(1)} %bitcast.34), channel_id=1, source_target_pairs={{0,32},{32,64},{64,96},{96,0},{1,33},{33,65},{65,97},{97,1},{2,34}... | collective-permute-start | bytes 786440 | tf_op jit(solution)/shard_map/ppermute | solution.py:30
  58.1 10.0 %collective-permute-start.1 = (bf16[128,1024]{1,0:T(8,128)(2,1)S(1)}, bf16[128,1024]{1,0:T(8,128)(2,1)S(1)}, u32[]{:S(2)}, u32[]{:S(2)}) collective-permute-start(bf16[128,1024]{1,0:T(8,128)(2,1)S(1)} %bitcast.35), channel_id=1, source_target_pairs={{0,64},{32,96},{64,0},{96,32},{1,65},{33,97},{65,1},{97,33},{2,66}... | collective-permute-start | bytes 786440 | tf_op jit(solution)/shard_map/ppermute | solution.py:30
  62.5 8.9 %collective-permute-start = (bf16[128,1024]{1,0:T(8,128)(2,1)S(1)}, bf16[128,1024]{1,0:T(8,128)(2,1)S(1)}, u32[]{:S(2)}, u32[]{:S(2)}) collective-permute-start(bf16[128,1024]{1,0:T(8,128)(2,1)S(1)} %bitcast.36), channel_id=1, source_target_pairs={{0,96},{32,0},{64,32},{96,64},{1,97},{33,1},{65,33},{97,65},{2,98}... | collective-permute-start | bytes 786440 | tf_op jit(solution)/shard_map/ppermute | solution.py:30
  71.5 1.7 copy-start.4
  72.3 44.8 %copy-start.2 = (f32[512,512]{1,0:T(8,128)}, f32[512,512]{1,0:T(8,128)S(1)}, u32[]{:S(2)}) copy-start(f32[512,512]{1,0:T(8,128)S(1)} %get-tuple-element.31) | copy-start | bytes 3145732
  72.3 1.6 copy-start
  73.9 14.2 %collective-permute-start.4 = (f32[8,128]{1,0:T(8,128)S(1)}, f32[8,128]{1,0:T(8,128)S(1)}, u32[]{:S(2)}, u32[]{:S(2)}) collective-permute-start(f32[8,128]{1,0:T(8,128)S(1)} %pad_maximum_fusion.6), channel_id=1, source_target_pairs={{0,1},{1,0},{2,3},{3,2},{4,5},{5,4},{6,7},{7,6},{8,9},{9,8},{10,11... | collective-permute-start | bytes 12296 | tf_op jit(solution)/shard_map/ppermute | solution.py:25
  81.1 16.0 %all-to-all-start.2 = ((f32[16,4,128]{2,1,0:T(4,128)}), f32[16,4,128]{2,1,0:T(4,128)S(1)}, u32[]{:S(2)}, u32[]{:S(2)}) async-start(f32[16,4,128]{2,1,0:T(4,128)} %broadcast_in_dim.115), calls=%async_computation.2 | async-start | bytes 65536 | tf_op jit(solution)/shard_map/all_to_all | solution.py:17
  99.1 12.5 %all-to-all-start.3 = ((f32[16,16,128]{2,1,0:T(8,128)}), f32[16,16,128]{2,1,0:T(8,128)S(1)}, u32[]{:S(2)}, u32[]{:S(2)}) async-start(f32[16,16,128]{2,1,0:T(8,128)} %broadcast_in_dim.120), calls=%async_computation.3 | async-start | bytes 262144 | tf_op jit(solution)/shard_map/all_to_all | solution.py:17
  117.2 2.2 %copy-start.1 = (bf16[512,1024]{1,0:T(8,128)(2,1)S(1)}, bf16[512,1024]{1,0:T(8,128)(2,1)}, u32[]{:S(2)}) copy-start(bf16[512,1024]{1,0:T(8,128)(2,1)} %copy-done) | copy-start | bytes 3145732
  120.2 11.3 %copy-start.5 = (bf16[512,1024]{1,0:T(8,128)(2,1)S(1)}, bf16[512,1024]{1,0:T(8,128)(2,1)}, u32[]{:S(2)}) copy-start(bf16[512,1024]{1,0:T(8,128)(2,1)} %copy-done.4) | copy-start | bytes 3145732
  122.5 16.3 %collective-permute-start.5 = (bf16[128,1152]{1,0:T(8,128)(2,1)S(1)}, bf16[128,1152]{1,0:T(8,128)(2,1)S(1)}, u32[]{:S(2)}, u32[]{:S(2)}) collective-permute-start(bf16[128,1152]{1,0:T(8,128)(2,1)S(1)} %get-tuple-element.20), channel_id=1, source_target_pairs={{0,32},{32,64},{64,96},{96,0},{1,33},{33,65},{65,97},{97,1},{2,34}... | collective-permute-start | bytes 884744 | tf_op jit(solution)/shard_map/ppermute | solution.py:30
  124.6 14.7 %collective-permute-start.6 = (bf16[128,1152]{1,0:T(8,128)(2,1)S(1)}, bf16[128,1152]{1,0:T(8,128)(2,1)S(1)}, u32[]{:S(2)}, u32[]{:S(2)}) collective-permute-start(bf16[128,1152]{1,0:T(8,128)(2,1)S(1)} %get-tuple-element.19), channel_id=1, source_target_pairs={{0,64},{32,96},{64,0},{96,32},{1,65},{33,97},{65,1},{97,33},{2,66}... | collective-permute-start | bytes 884744 | tf_op jit(solution)/shard_map/ppermute | solution.py:30
  128.3 13.7 %collective-permute-start.7 = (bf16[128,1152]{1,0:T(8,128)(2,1)}, bf16[128,1152]{1,0:T(8,128)(2,1)S(1)}, u32[]{:S(2)}, u32[]{:S(2)}) collective-permute-start(bf16[128,1152]{1,0:T(8,128)(2,1)} %get-tuple-element.18), channel_id=1, source_target_pairs={{0,96},{32,0},{64,32},{96,64},{1,97},{33,1},{65,33},{97,65},{2,98}... | collective-permute-start | bytes 884744 | tf_op jit(solution)/shard_map/ppermute | solution.py:30
  133.4 24.7 %copy-start.3 = (f32[512,512]{1,0:T(8,128)S(1)}, f32[512,512]{1,0:T(8,128)}, u32[]{:S(2)}) copy-start(f32[512,512]{1,0:T(8,128)} %copy-done.2) | copy-start | bytes 3145732
  133.4 24.7 %collective-permute-start.9 = (bf16[512,1024]{1,0:T(8,128)(2,1)}, bf16[512,1024]{1,0:T(8,128)(2,1)}, u32[]{:S(2)}, u32[]{:S(2)}) collective-permute-start(bf16[512,1024]{1,0:T(8,128)(2,1)} %convolution_convert_fusion), channel_id=1, source_target_pairs={{0,1},{1,0},{2,3},{3,2},{4,5},{5,4},{6,7},{7,6},{8,9},{9,8},{10,11... | collective-permute-start | bytes 3145736 | tf_op jit(solution)/shard_map/ppermute | solution.py:25
  138.7 0.7 copy-start.10
  139.5 0.7 copy-start.11
  142.1 5.8 %copy-start.12 = (bf16[128,1152]{1,0:T(8,128)(2,1)}, bf16[128,1152]{1,0:T(8,128)(2,1)S(1)}, u32[]{:S(2)}) copy-start(bf16[128,1152]{1,0:T(8,128)(2,1)S(1)} %collective-permute-done.7) | copy-start | bytes 884740
  143.4 5.7 %collective-permute-start.8 = (f32[8,128]{1,0:T(8,128)S(1)}, f32[8,128]{1,0:T(8,128)S(1)}, u32[]{:S(2)}, u32[]{:S(2)}) collective-permute-start(f32[8,128]{1,0:T(8,128)S(1)} %broadcast_in_dim.124), channel_id=1, source_target_pairs={{0,1},{1,0},{2,3},{3,2},{4,5},{5,4},{6,7},{7,6},{8,9},{9,8},{10,11... | collective-permute-start | bytes 12296 | tf_op jit(solution)/shard_map/ppermute | solution.py:25
  154.7 13.8 %all-to-all-start.4 = ((bf16[4,32,1152]{2,1,0:T(8,128)(2,1)}), bf16[4,32,1152]{2,1,0:T(8,128)(2,1)S(1)}, u32[]{:S(2)}, u32[]{:S(2)}) async-start(bf16[4,32,1152]{2,1,0:T(8,128)(2,1)} %pad_maximum_fusion.4), calls=%async_computation.4 | async-start | bytes 589824 | tf_op jit(solution)/shard_map/all_to_all | solution.py:17
  161.6 36.8 %copy-start.8 = (f32[32,1024]{1,0:T(8,128)S(1)}, f32[32,1024]{1,0:T(8,128)}, u32[]{:S(2)}) copy-start(f32[32,1024]{1,0:T(8,128)} %get-tuple-element.30) | copy-start | bytes 393220
  168.5 29.7 %all-to-all-start.5 = ((bf16[16,32,1024]{2,1,0:T(8,128)(2,1)}), bf16[16,32,1024]{2,1,0:T(8,128)(2,1)S(1)}, u32[]{:S(2)}, u32[]{:S(2)}) async-start(bf16[16,32,1024]{2,1,0:T(8,128)(2,1)} %bitcast.14), calls=%async_computation.5 | async-start | bytes 2097152 | tf_op jit(solution)/shard_map/all_to_all | solution.py:17
where the time goes:
time: 202 us; the launch traced here: 200 us
  waiting for transfers between devices  80.4 us (40%)
  starting transfers between devices  76.7 us (38%)
  between operations  12.8 us (6%)
  matrix products  12.4 us (6%)
  other arithmetic  11.8 us (6%)
  local copies, waits for them, and re-layouts  6.07 us (3%)
    all_to_all x6, waiting for transfers between devices, exchange(): return lax.all_to_all(blocks, axes, 0, 0, tiled=True)  74.7 us
    all_to_all x6, starting transfers between devices, exchange(): return lax.all_to_all(blocks, axes, 0, 0, tiled=True)  36.5 us
    ppermute x4, starting transfers between devices, swap_core(): return lax.ppermute(x, 'core', [(0, 1), (1, 0)])  20.6 us
    ppermute x6, starting transfers between devices, shift_x(): return lax.ppermute(x, 'x', [(i, (i + d) % n) for i in range(n)])  19.6 us
    ppermute x6, waiting for transfers between devices, shift_x(): return lax.ppermute(x, 'x', [(i, (i + d) % n) for i in range(n)])  5.75 us
  transfers between devices with their start and end apart: 16, of which 8 were waited for; matrix products, arithmetic and copies ran while one was open for 8% of the time, Pallas kernels for 0%

commit v1 on v0

--- a/solution.py
+++ b/solution.py
@@ -46,13 +46,9 @@
     return peak + jnp.log(jnp.exp(a - peak) + jnp.exp(b - peak))
 
 
-def lanes_of(x, rows):
-    hi = lax.reduce_precision(x, 8, 7)
-    mid = lax.reduce_precision(x - hi, 8, 7)
-    low = x - hi - mid
-    lane = lax.broadcasted_iota(jnp.int32, (rows, LANES), 1)
-    zero = jnp.zeros((rows, LANES), jnp.float32)
-    return jnp.where(lane == 0, hi, jnp.where(lane == 1, mid, jnp.where(lane == 2, low, zero)))
+def add_partner(x, axis, step):
+    n = lax.axis_size(axis)
+    return x + lax.ppermute(x, axis, [(i, i ^ step) for i in range(n)])
 
 
 def inner(query, passage, positive):
@@ -68,7 +64,9 @@
     near = exchange(spread(passage, n_yh), "yh").reshape(n_yh * rows, embed)
     own = exchange(spread(query, n_chip), CHIP_AXES).reshape(half, embed)
     far = [shift_x(near, n_x - d) for d in range(1, n_x)]
-    pall = lax.optimization_barrier(jnp.concatenate([near] + far, axis=0))
+    ring = jnp.stack([near] + far + [near] + far[:-1])
+    pall = lax.dynamic_slice_in_dim(ring, (n_x - x_at) % n_x, n_x, 0)
+    pall = lax.optimization_barrier(pall.reshape(n_p, embed))
     other = swap_core(own)
 
     slot = jnp.arange(rows, dtype=jnp.int32)
@@ -89,12 +87,8 @@
         jnp.exp(s0 - col_peak[None, :]).sum(axis=0) + jnp.exp(s1 - col_peak[None, :]).sum(axis=0)
     )
 
-    place = jnp.arange(n_x, dtype=jnp.int32)
-    moved = ((place[:, None] - x_at + n_x) % n_x == place[None, :])[:, :, None]
-    col_part = jnp.where(moved, col_part.reshape(1, n_x, n_yh * rows), 0.0).sum(axis=1)
     col_all = exchange(spread(col_part.reshape(-1, LANES), n_pass), PASS_AXES)
-    col_lse = lse(col_all, 0).reshape(n_x, 1, n_yh * rows)
-    col_lse = jnp.where(moved, col_lse, 0.0).sum(axis=0).reshape(n_p)
+    col_lse = lse(col_all, 0).reshape(n_p)
 
     k = half // LANES
     pair = lse2(rows_mine, jnp.concatenate([rows_theirs[k:], rows_theirs[:k]], axis=0))
@@ -113,31 +107,24 @@
 
     w1 = weights(s1, row_lse1)
     w0 = weights(s0, row_lse0)
-    given = jnp.dot(w1, pall, preferred_element_type=jnp.float32).astype(jnp.bfloat16)
-    taken = swap_core(given)
-    qgrad = jnp.dot(w0, pall, preferred_element_type=jnp.float32) + taken.astype(jnp.float32)
-    qgrad = exchange(qgrad.astype(jnp.bfloat16).reshape(n_chip, rows, embed), CHIP_AXES)
-
     tn = (((0,), (0,)), ((), ()))
     pgrad = lax.dot_general(w0, own, tn, preferred_element_type=jnp.float32) + lax.dot_general(
         w1, other, tn, preferred_element_type=jnp.float32
     )
-    pgrad = pgrad.reshape(n_x, n_yh * rows, embed)
+    pgrad = exchange(pgrad.astype(jnp.bfloat16).reshape(n_pass, rows, embed), PASS_AXES)
+    given = jnp.dot(w1, pall, preferred_element_type=jnp.float32).astype(jnp.bfloat16)
+    taken = swap_core(given)
+    qgrad = jnp.dot(w0, pall, preferred_element_type=jnp.float32) + taken.astype(jnp.float32)
+    qgrad = qgrad.astype(jnp.bfloat16)
+    qgrad = exchange(qgrad.reshape(n_chip, rows, embed), CHIP_AXES)
+    part = add_partner(jnp.broadcast_to(part, (8, LANES)), "core", 1)
+    part = add_partner(part, "x", 1)
+    part = add_partner(part, "x", 2)
+    part = add_partner(part, "yh", 1)
+    part = add_partner(part, "yh", 2)
+    loss = part[0, 0] / (2.0 * n_pass * n_chip * 2 * rows)
 
-    def with_lanes(block, value):
-        return jnp.concatenate([block, lanes_of(value, block.shape[0])], axis=1).astype(
-            jnp.bfloat16
-        )
-
-    got = [shift_x(with_lanes(pgrad[d], part), d) for d in range(1, n_x)]
-    mid = pgrad[0] + sum(g[:, :embed].astype(jnp.float32) for g in got)
-    part = part + sum(g[0, embed:].astype(jnp.float32).sum() for g in got)
-    part = part + swap_core(jnp.broadcast_to(part, (8, LANES)))[0, 0]
-    mid = exchange(with_lanes(mid, part).reshape(n_yh, rows, embed + LANES), "yh")
-    passage_sum = mid[:, :, :embed].astype(jnp.float32).sum(axis=0)
-    part = mid[:, 0, embed:].astype(jnp.float32).sum()
-    loss = part / (2.0 * n_pass * n_chip * 2 * rows)
-
+    passage_sum = pgrad.astype(jnp.float32).sum(axis=0)
     query_sum = qgrad.astype(jnp.float32).sum(axis=0)
     grad_query = (logit_scale * (query_sum - paired_passage)).astype(jnp.bfloat16)
     grad_passage = (logit_scale * (passage_sum - paired_query)).astype(jnp.bfloat16)

time: 202 us -> 178 us (0.88)
  the two profiles are of different devices: /device:TPU:1 before, /device:TPU:8 now
where the time goes in v1:
time: 178 us; the launch traced here: 177 us
  waiting for transfers between devices  69.8 us (39%)
  starting transfers between devices  62.8 us (35%)
  blocking collectives  12.4 us (7%)
  local copies, waits for them, and re-layouts  11.8 us (7%)
  matrix products  11.5 us (6%)
  between operations  5.33 us (3%)
  other arithmetic  3.79 us (2%)
    all_to_all x5, waiting for transfers between devices, exchange(): return lax.all_to_all(blocks, axes, 0, 0, tiled=True)  42 us
    all_to_all x5, starting transfers between devices, exchange(): return lax.all_to_all(blocks, axes, 0, 0, tiled=True)  34 us
    ppermute x5, waiting for transfers between devices, add_partner(): return x + lax.ppermute(x, axis, [(i, i ^ step) for i in range(n)])  19.5 us
    all_to_all x1, blocking collectives, exchange(): return lax.all_to_all(blocks, axes, 0, 0, tiled=True)  12.4 us
    ppermute x5, starting transfers between devices, add_partner(): return x + lax.ppermute(x, axis, [(i, i ^ step) for i in range(n)])  11.8 us
    ppermute x3, starting transfers between devices, shift_x(): return lax.ppermute(x, 'x', [(i, (i + d) % n) for i in range(n)])  10.8 us
    ppermute x3, starting transfers between devices, swap_core(): return lax.ppermute(x, 'core', [(0, 1), (1, 0)])  6.24 us
    ppermute x3, waiting for transfers between devices, shift_x(): return lax.ppermute(x, 'x', [(i, (i + d) % n) for i in range(n)])  5.64 us
  transfers between devices with their start and end apart: 16, of which 11 were waited for; matrix products, arithmetic and copies ran while one was open for 10% of the time, Pallas kernels for 0%

profile of v1, /device:TPU:8, one launch (start us, length us, event | category | flops | bytes accessed | tf_op | source)
XLA Modules:
  0.0 177.4 jit_solution(15093980956699917394)
XLA Ops:
  0.6 1.6 broadcast_in_dim.21
  2.2 6.3 %all-to-all-start = ((bf16[4,32,1024]{2,1,0:T(8,128)(2,1)}), bf16[4,32,1024]{2,1,0:T(8,128)(2,1)S(1)}, u32[]{:S(2)}, u32[]{:S(2)}) async-start(bf16[4,32,1024]{2,1,0:T(8,128)(2,1)} %broadcast_in_dim.21), calls=%async_computation | async-start | bytes 524288 | tf_op jit(solution)/shard_map/all_to_all | solution.py:17
  8.5 2.0 %broadcast_in_dim.23 = bf16[16,32,1024]{2,1,0:T(8,128)(2,1)} broadcast(bf16[32,1024]{1,0:T(8,128)(2,1)} %param.3), dimensions={1,2} | broadcast | bytes 1114112 | tf_op jit(solution)/shard_map/broadcast_in_dim | solution.py:21
  10.5 8.0 %all-to-all-done = bf16[4,32,1024]{2,1,0:T(8,128)(2,1)S(1)} async-done(((bf16[4,32,1024]{2,1,0:T(8,128)(2,1)}), bf16[4,32,1024]{2,1,0:T(8,128)(2,1)S(1)}, u32[]{:S(2)}, u32[]{:S(2)}) %all-to-all-start) | async-done | bytes 262176 | tf_op jit(solution)/shard_map/all_to_all | solution.py:17
  18.5 12.1 %all-to-all-start.1 = ((bf16[16,32,1024]{2,1,0:T(8,128)(2,1)}), bf16[16,32,1024]{2,1,0:T(8,128)(2,1)S(1)}, u32[]{:S(2)}, u32[]{:S(2)}) async-start(bf16[16,32,1024]{2,1,0:T(8,128)(2,1)} %broadcast_in_dim.23), calls=%async_computation.1 | async-start | bytes 2097152 | tf_op jit(solution)/shard_map/all_to_all | solution.py:17
  30.6 4.7 %collective-permute-start = (bf16[128,1024]{1,0:T(8,128)(2,1)S(1)}, bf16[128,1024]{1,0:T(8,128)(2,1)S(1)}, u32[]{:S(2)}, u32[]{:S(2)}) collective-permute-start(bf16[128,1024]{1,0:T(8,128)(2,1)S(1)} %bitcast.45), channel_id=1, source_target_pairs={{0,96},{32,0},{64,32},{96,64},{1,97},{33,1},{65,33},{97,65},{2,98}... | collective-permute-start | bytes 786440 | tf_op jit(solution)/shard_map/ppermute | solution.py:30
  35.3 0.8 multiply_reduce_fusion
  36.8 1.9 %collective-permute-start.2 = (bf16[128,1024]{1,0:T(8,128)(2,1)S(1)}, bf16[128,1024]{1,0:T(8,128)(2,1)S(1)}, u32[]{:S(2)}, u32[]{:S(2)}) collective-permute-start(bf16[128,1024]{1,0:T(8,128)(2,1)S(1)} %bitcast.46), channel_id=1, source_target_pairs={{0,32},{32,64},{64,96},{96,0},{1,33},{33,65},{65,97},{97,1},{2,34}... | collective-permute-start | bytes 786440 | tf_op jit(solution)/shard_map/ppermute | solution.py:30
  38.7 4.2 %collective-permute-start.1 = (bf16[128,1024]{1,0:T(8,128)(2,1)S(1)}, bf16[128,1024]{1,0:T(8,128)(2,1)S(1)}, u32[]{:S(2)}, u32[]{:S(2)}) collective-permute-start(bf16[128,1024]{1,0:T(8,128)(2,1)S(1)} %bitcast.47), channel_id=1, source_target_pairs={{0,64},{32,96},{64,0},{96,32},{1,65},{33,97},{65,1},{97,33},{2,66}... | collective-permute-start | bytes 786440 | tf_op jit(solution)/shard_map/ppermute | solution.py:30
  42.9 0.7 bitcast_dynamic-update-slice_fusion.5
  43.6 0.7 bitcast_dynamic-update-slice_fusion.3
  44.3 5.6 %collective-permute-done.1 = bf16[128,1024]{1,0:T(8,128)(2,1)S(1)} collective-permute-done((bf16[128,1024]{1,0:T(8,128)(2,1)S(1)}, bf16[128,1024]{1,0:T(8,128)(2,1)S(1)}, u32[]{:S(2)}, u32[]{:S(2)}) %collective-permute-start.1) | collective-permute-done | bytes 262176 | tf_op jit(solution)/shard_map/ppermute | solution.py:30
  49.9 0.7 bitcast_dynamic-update-slice_fusion.1
  50.7 4.8 %all-to-all-done.1 = bf16[16,32,1024]{2,1,0:T(8,128)(2,1)S(1)} async-done(((bf16[16,32,1024]{2,1,0:T(8,128)(2,1)}), bf16[16,32,1024]{2,1,0:T(8,128)(2,1)S(1)}, u32[]{:S(2)}, u32[]{:S(2)}) %all-to-all-start.1) | async-done | bytes 1048608 | tf_op jit(solution)/shard_map/all_to_all | solution.py:17
  55.5 1.9 %collective-permute-start.3 = (bf16[512,1024]{1,0:T(8,128)(2,1)S(1)}, bf16[512,1024]{1,0:T(8,128)(2,1)S(1)}, u32[]{:S(2)}, u32[]{:S(2)}) collective-permute-start(bf16[512,1024]{1,0:T(8,128)(2,1)S(1)} %bitcast.54), channel_id=1, source_target_pairs={{0,1},{1,0},{2,3},{3,2},{4,5},{5,4},{6,7},{7,6},{8,9},{9,8},{10,11... | collective-permute-start | bytes 3145736 | tf_op jit(solution)/shard_map/ppermute | solution.py:25
  57.4 0.7 bitcast_dynamic-update-slice_fusion
  58.1 0.7 bitcast_dynamic-update-slice_fusion.6
  58.9 0.7 bitcast_dynamic-update-slice_fusion.4
  59.6 0.7 bitcast_dynamic-update-slice_fusion.2
  60.3 1.3 constant_dynamic-slice_fusion
  61.6 0.8 fusion.10
  62.5 0.8 fusion.11
  63.4 0.7 exponential_reduce_fusion.2
  64.2 2.4 %collective-permute-start.4 = (f32[8,128]{1,0:T(8,128)S(1)}, f32[8,128]{1,0:T(8,128)S(1)}, u32[]{:S(2)}, u32[]{:S(2)}) collective-permute-start(f32[8,128]{1,0:T(8,128)S(1)} %pad_maximum_fusion.1), channel_id=1, source_target_pairs={{0,1},{1,0},{2,3},{3,2},{4,5},{5,4},{6,7},{7,6},{8,9},{9,8},{10,11... | collective-permute-start | bytes 12296 | tf_op jit(solution)/shard_map/ppermute | solution.py:25
  67.2 8.3 %all-to-all-start.2 = ((f32[16,4,128]{2,1,0:T(4,128)}), f32[16,4,128]{2,1,0:T(4,128)S(1)}, u32[]{:S(2)}, u32[]{:S(2)}) async-start(f32[16,4,128]{2,1,0:T(4,128)} %broadcast_in_dim.24), calls=%async_computation.2 | async-start | bytes 65536 | tf_op jit(solution)/shard_map/all_to_all | solution.py:17
  75.5 10.0 %all-to-all-done.2 = f32[16,4,128]{2,1,0:T(4,128)S(1)} async-done(((f32[16,4,128]{2,1,0:T(4,128)}), f32[16,4,128]{2,1,0:T(4,128)S(1)}, u32[]{:S(2)}, u32[]{:S(2)}) %all-to-all-start.2) | async-done | bytes 32800 | tf_op jit(solution)/shard_map/all_to_all | solution.py:17
  86.2 0.6 broadcast_select_fusion
  86.8 12.4 %all_to_all.30 = f32[16,16,128]{2,1,0:T(8,128)S(1)} all-to-all(f32[16,16,128]{2,1,0:T(8,128)S(1)} %broadcast_in_dim.28), channel_id=1, replica_groups=mesh['yh'=4,'x'=4,'z'=8,'yl'=2,'core'=2] {'z','yl'}, dimensions={0} | all-to-all | bytes 262144 | tf_op jit(solution)/shard_map/all_to_all | solution.py:17
  99.9 2.2 %fusion.9 = f32[512,1024]{1,0:T(8,128)S(1)} fusion(bf16[512,1024]{1,0:T(8,128)(2,1)} %bitcast.56, f32[512,512]{1,0:T(8,128)S(1)} %get-tuple-element.25, f32[512]{0:T(512)S(1)} %get-tuple-element.15, f32[512]{0:T(512)S(1)} %get-tuple-element.13), kind=kOutput, calls=%fused_computation.53 | convolution fusion | flops 538181632 | bytes 4198400 | tf_op jit(solution)/shard_map/dot_general | solution.py:111
  102.1 1.9 %add_convert_fusion = bf16[512,1024]{1,0:T(8,128)(2,1)} fusion(f32[512,1024]{1,0:T(8,128)S(1)} %fusion.9, bf16[512,1024]{1,0:T(8,128)(2,1)S(1)} %copy-done.6, f32[512,512]{1,0:T(8,128)S(1)} %get-tuple-element.26, f32[512]{0:T(512)S(1)} %get-tuple-element.14, f32[512]{0:T(512)S(1)} %get-tuple-element.15), kind=kOutput, calls=%fused_computation.1 | convolution fusion | flops 539230208 | bytes 5246976 | tf_op jit(solution)/shard_map/dot_general | solution.py:111
  104.0 3.7 %all-to-all-start.5 = ((bf16[16,32,1024]{2,1,0:T(8,128)(2,1)}), bf16[16,32,1024]{2,1,0:T(8,128)(2,1)S(1)}, u32[]{:S(2)}, u32[]{:S(2)}) async-start(bf16[16,32,1024]{2,1,0:T(8,128)(2,1)} %bitcast.58), calls=%async_computation.5 | async-start | bytes 2097152 | tf_op jit(solution)/shard_map/all_to_all | solution.py:17
  107.7 2.1 %convolution_convert_fusion = bf16[512,1024]{1,0:T(8,128)(2,1)S(1)} fusion(bf16[512,1024]{1,0:T(8,128)(2,1)S(1)} %bitcast.52, f32[512,512]{1,0:T(8,128)} %copy-done, f32[512]{0:T(512)S(1)} %get-tuple-element.14, f32[512]{0:T(512)S(1)} %get-tuple-element.15), kind=kOutput, calls=%fused_computation.4 | convolution fusion | flops 538705920 | bytes 3149824 | tf_op jit(solution)/shard_map/dot_general | solution.py:115
  109.8 1.9 %collective-permute-start.10 = (bf16[512,1024]{1,0:T(8,128)(2,1)S(1)}, bf16[512,1024]{1,0:T(8,128)(2,1)S(1)}, u32[]{:S(2)}, u32[]{:S(2)}) collective-permute-start(bf16[512,1024]{1,0:T(8,128)(2,1)S(1)} %convolution_convert_fusion), channel_id=1, source_target_pairs={{0,1},{1,0},{2,3},{3,2},{4,5},{5,4},{6,7},{7,6},{8,9},{9,8},{10,11... | collective-permute-start | bytes 3145736 | tf_op jit(solution)/shard_map/ppermute | solution.py:25
  111.7 2.6 %collective-permute-done.10 = bf16[512,1024]{1,0:T(8,128)(2,1)S(1)} collective-permute-done((bf16[512,1024]{1,0:T(8,128)(2,1)S(1)}, bf16[512,1024]{1,0:T(8,128)(2,1)S(1)}, u32[]{:S(2)}, u32[]{:S(2)}) %collective-permute-start.10) | collective-permute-done | bytes 1048608 | tf_op jit(solution)/shard_map/ppermute | solution.py:25
  114.3 1.9 %add_convert_fusion.1 = bf16[512,1024]{1,0:T(8,128)(2,1)} fusion(bf16[512,1024]{1,0:T(8,128)(2,1)S(1)} %collective-permute-done.10, bf16[512,1024]{1,0:T(8,128)(2,1)S(1)} %bitcast.53, f32[512,512]{1,0:T(8,128)S(1)} %get-tuple-element.25, f32[512]{0:T(512)S(1)} %get-tuple-element.15, f32[512]{0:T(512)S(1)} %get-tuple-element.13), kind=kOutput, calls=%fused_computation.3 | convolution fusion | flops 539754496 | bytes 4198400 | tf_op jit(solution)/shard_map/dot_general | solution.py:117
  116.2 19.3 %all-to-all-done.5 = bf16[16,32,1024]{2,1,0:T(8,128)(2,1)S(1)} async-done(((bf16[16,32,1024]{2,1,0:T(8,128)(2,1)}), bf16[16,32,1024]{2,1,0:T(8,128)(2,1)S(1)}, u32[]{:S(2)}, u32[]{:S(2)}) %all-to-all-start.5) | async-done | bytes 1048608 | tf_op jit(solution)/shard_map/all_to_all | solution.py:17
  135.5 3.7 %all-to-all-start.4 = ((bf16[16,32,1024]{2,1,0:T(8,128)(2,1)}), bf16[16,32,1024]{2,1,0:T(8,128)(2,1)S(1)}, u32[]{:S(2)}, u32[]{:S(2)}) async-start(bf16[16,32,1024]{2,1,0:T(8,128)(2,1)} %bitcast.57), calls=%async_computation.4 | async-start | bytes 2097152 | tf_op jit(solution)/shard_map/all_to_all | solution.py:17
  141.8 1.9 %collective-permute-start.5 = (f32[8,128]{1,0:T(8,128)S(1)}, f32[8,128]{1,0:T(8,128)S(1)}, u32[]{:S(2)}, u32[]{:S(2)}) collective-permute-start(f32[8,128]{1,0:T(8,128)S(1)} %broadcast_in_dim.52), channel_id=1, source_target_pairs={{0,1},{1,0},{2,3},{3,2},{4,5},{5,4},{6,7},{7,6},{8,9},{9,8},{10,11... | collective-permute-start | bytes 12296 | tf_op jit(solution)/shard_map/ppermute | solution.py:51
  143.7 1.1 collective-permute-done.5
  144.8 2.2 %collective-permute-start.6 = (f32[8,128]{1,0:T(8,128)S(1)}, f32[8,128]{1,0:T(8,128)S(1)}, u32[]{:S(2)}, u32[]{:S(2)}) collective-permute-start(f32[8,128]{1,0:T(8,128)S(1)} %broadcast_add_fusion), channel_id=1, source_target_pairs={{0,32},{32,0},{64,96},{96,64},{1,33},{33,1},{65,97},{97,65},{2,34}... | collective-permute-start | bytes 12296 | tf_op jit(solution)/shard_map/ppermute | solution.py:51
  147.1 3.3 %collective-permute-done.6 = f32[8,128]{1,0:T(8,128)S(1)} collective-permute-done((f32[8,128]{1,0:T(8,128)S(1)}, f32[8,128]{1,0:T(8,128)S(1)}, u32[]{:S(2)}, u32[]{:S(2)}) %collective-permute-start.6) | collective-permute-done | bytes 4128 | tf_op jit(solution)/shard_map/ppermute | solution.py:51
  150.3 2.7 %collective-permute-start.7 = (f32[8,128]{1,0:T(8,128)S(1)}, f32[8,128]{1,0:T(8,128)S(1)}, u32[]{:S(2)}, u32[]{:S(2)}) collective-permute-start(f32[8,128]{1,0:T(8,128)S(1)} %fusion.25), channel_id=1, source_target_pairs={{0,64},{32,96},{64,0},{96,32},{1,65},{33,97},{65,1},{97,33},{2,66}... | collective-permute-start | bytes 12296 | tf_op jit(solution)/shard_map/ppermute | solution.py:51
  153.0 4.3 %collective-permute-done.7 = f32[8,128]{1,0:T(8,128)S(1)} collective-permute-done((f32[8,128]{1,0:T(8,128)S(1)}, f32[8,128]{1,0:T(8,128)S(1)}, u32[]{:S(2)}, u32[]{:S(2)}) %collective-permute-start.7) | collective-permute-done | bytes 4128 | tf_op jit(solution)/shard_map/ppermute | solution.py:51
  157.3 2.4 %collective-permute-start.8 = (f32[8,128]{1,0:T(8,128)S(1)}, f32[8,128]{1,0:T(8,128)S(1)}, u32[]{:S(2)}, u32[]{:S(2)}) collective-permute-start(f32[8,128]{1,0:T(8,128)S(1)} %add.112), channel_id=1, source_target_pairs={{0,128},{128,0},{256,384},{384,256},{1,129},{129,1},{257,385},{385... | collective-permute-start | bytes 12296 | tf_op jit(solution)/shard_map/ppermute | solution.py:51
  159.7 4.0 %collective-permute-done.8 = f32[8,128]{1,0:T(8,128)S(1)} collective-permute-done((f32[8,128]{1,0:T(8,128)S(1)}, f32[8,128]{1,0:T(8,128)S(1)}, u32[]{:S(2)}, u32[]{:S(2)}) %collective-permute-start.8) | collective-permute-done | bytes 4128 | tf_op jit(solution)/shard_map/ppermute | solution.py:51
  163.7 2.5 %collective-permute-start.9 = (f32[8,128]{1,0:T(8,128)S(1)}, f32[8,128]{1,0:T(8,128)S(1)}, u32[]{:S(2)}, u32[]{:S(2)}) collective-permute-start(f32[8,128]{1,0:T(8,128)S(1)} %add.113), channel_id=1, source_target_pairs={{0,256},{128,384},{256,0},{384,128},{1,257},{129,385},{257,1},{385... | collective-permute-start | bytes 12296 | tf_op jit(solution)/shard_map/ppermute | solution.py:51
  166.3 6.9 %collective-permute-done.9 = f32[8,128]{1,0:T(8,128)S(1)} collective-permute-done((f32[8,128]{1,0:T(8,128)S(1)}, f32[8,128]{1,0:T(8,128)S(1)}, u32[]{:S(2)}, u32[]{:S(2)}) %collective-permute-start.9) | collective-permute-done | bytes 4128 | tf_op jit(solution)/shard_map/ppermute | solution.py:51
  174.5 0.9 fusion.1
  (50 shorter events, 4.4 us)
Async XLA Ops:
  2.2 33.1 %copy-start.2 = (bf16[32,1024]{1,0:T(8,128)(2,1)S(1)}, bf16[32,1024]{1,0:T(8,128)(2,1)}, u32[]{:S(2)}) copy-start(bf16[32,1024]{1,0:T(8,128)(2,1)} %param.3) | copy-start | bytes 196612
  2.2 33.1 %copy-start.3 = (bf16[32,1024]{1,0:T(8,128)(2,1)S(1)}, bf16[32,1024]{1,0:T(8,128)(2,1)}, u32[]{:S(2)}) copy-start(bf16[32,1024]{1,0:T(8,128)(2,1)} %param.4) | copy-start | bytes 196612
  2.2 33.1 %copy-start.4 = (s32[1,32]{1,0:T(1,128)S(1)}, s32[1,32]{1,0:T(1,128)}, u32[]{:S(2)}) copy-start(s32[1,32]{1,0:T(1,128)} %param.5) | copy-start | bytes 388
  2.2 16.3 %all-to-all-start = ((bf16[4,32,1024]{2,1,0:T(8,128)(2,1)}), bf16[4,32,1024]{2,1,0:T(8,128)(2,1)S(1)}, u32[]{:S(2)}, u32[]{:S(2)}) async-start(bf16[4,32,1024]{2,1,0:T(8,128)(2,1)} %broadcast_in_dim.21), calls=%async_computation | async-start | bytes 524288 | tf_op jit(solution)/shard_map/all_to_all | solution.py:17
  18.5 37.0 %all-to-all-start.1 = ((bf16[16,32,1024]{2,1,0:T(8,128)(2,1)}), bf16[16,32,1024]{2,1,0:T(8,128)(2,1)S(1)}, u32[]{:S(2)}, u32[]{:S(2)}) async-start(bf16[16,32,1024]{2,1,0:T(8,128)(2,1)} %broadcast_in_dim.23), calls=%async_computation.1 | async-start | bytes 2097152 | tf_op jit(solution)/shard_map/all_to_all | solution.py:17
  30.6 13.0 %collective-permute-start = (bf16[128,1024]{1,0:T(8,128)(2,1)S(1)}, bf16[128,1024]{1,0:T(8,128)(2,1)S(1)}, u32[]{:S(2)}, u32[]{:S(2)}) collective-permute-start(bf16[128,1024]{1,0:T(8,128)(2,1)S(1)} %bitcast.45), channel_id=1, source_target_pairs={{0,96},{32,0},{64,32},{96,64},{1,97},{33,1},{65,33},{97,65},{2,98}... | collective-permute-start | bytes 786440 | tf_op jit(solution)/shard_map/ppermute | solution.py:30
  36.8 20.6 %collective-permute-start.2 = (bf16[128,1024]{1,0:T(8,128)(2,1)S(1)}, bf16[128,1024]{1,0:T(8,128)(2,1)S(1)}, u32[]{:S(2)}, u32[]{:S(2)}) collective-permute-start(bf16[128,1024]{1,0:T(8,128)(2,1)S(1)} %bitcast.46), channel_id=1, source_target_pairs={{0,32},{32,64},{64,96},{96,0},{1,33},{33,65},{65,97},{97,1},{2,34}... | collective-permute-start | bytes 786440 | tf_op jit(solution)/shard_map/ppermute | solution.py:30
  38.7 11.3 %collective-permute-start.1 = (bf16[128,1024]{1,0:T(8,128)(2,1)S(1)}, bf16[128,1024]{1,0:T(8,128)(2,1)S(1)}, u32[]{:S(2)}, u32[]{:S(2)}) collective-permute-start(bf16[128,1024]{1,0:T(8,128)(2,1)S(1)} %bitcast.47), channel_id=1, source_target_pairs={{0,64},{32,96},{64,0},{96,32},{1,65},{33,97},{65,1},{97,33},{2,66}... | collective-permute-start | bytes 786440 | tf_op jit(solution)/shard_map/ppermute | solution.py:30
  55.5 6.2 %copy-start.1 = (bf16[16,32,1024]{2,1,0:T(8,128)(2,1)}, bf16[16,32,1024]{2,1,0:T(8,128)(2,1)S(1)}, u32[]{:S(2)}) copy-start(bf16[16,32,1024]{2,1,0:T(8,128)(2,1)S(1)} %all-to-all-done.1) | copy-start | bytes 3145732
  55.5 7.0 %collective-permute-start.3 = (bf16[512,1024]{1,0:T(8,128)(2,1)S(1)}, bf16[512,1024]{1,0:T(8,128)(2,1)S(1)}, u32[]{:S(2)}, u32[]{:S(2)}) collective-permute-start(bf16[512,1024]{1,0:T(8,128)(2,1)S(1)} %bitcast.54), channel_id=1, source_target_pairs={{0,1},{1,0},{2,3},{3,2},{4,5},{5,4},{6,7},{7,6},{8,9},{9,8},{10,11... | collective-permute-start | bytes 3145736 | tf_op jit(solution)/shard_map/ppermute | solution.py:25
  62.4 1.0 copy-start.5
  63.4 38.6 %copy-start = (f32[512,512]{1,0:T(8,128)}, f32[512,512]{1,0:T(8,128)S(1)}, u32[]{:S(2)}) copy-start(f32[512,512]{1,0:T(8,128)S(1)} %get-tuple-element.26) | copy-start | bytes 3145732
  64.2 11.3 %collective-permute-start.4 = (f32[8,128]{1,0:T(8,128)S(1)}, f32[8,128]{1,0:T(8,128)S(1)}, u32[]{:S(2)}, u32[]{:S(2)}) collective-permute-start(f32[8,128]{1,0:T(8,128)S(1)} %pad_maximum_fusion.1), channel_id=1, source_target_pairs={{0,1},{1,0},{2,3},{3,2},{4,5},{5,4},{6,7},{7,6},{8,9},{9,8},{10,11... | collective-permute-start | bytes 12296 | tf_op jit(solution)/shard_map/ppermute | solution.py:25
  67.2 18.3 %all-to-all-start.2 = ((f32[16,4,128]{2,1,0:T(4,128)}), f32[16,4,128]{2,1,0:T(4,128)S(1)}, u32[]{:S(2)}, u32[]{:S(2)}) async-start(f32[16,4,128]{2,1,0:T(4,128)} %broadcast_in_dim.24), calls=%async_computation.2 | async-start | bytes 65536 | tf_op jit(solution)/shard_map/all_to_all | solution.py:17
  99.9 2.2 %copy-start.6 = (bf16[512,1024]{1,0:T(8,128)(2,1)S(1)}, bf16[512,1024]{1,0:T(8,128)(2,1)}, u32[]{:S(2)}) copy-start(bf16[512,1024]{1,0:T(8,128)(2,1)} %copy-done.5) | copy-start | bytes 3145732
  104.0 31.5 %all-to-all-start.5 = ((bf16[16,32,1024]{2,1,0:T(8,128)(2,1)}), bf16[16,32,1024]{2,1,0:T(8,128)(2,1)S(1)}, u32[]{:S(2)}, u32[]{:S(2)}) async-start(bf16[16,32,1024]{2,1,0:T(8,128)(2,1)} %bitcast.58), calls=%async_computation.5 | async-start | bytes 2097152 | tf_op jit(solution)/shard_map/all_to_all | solution.py:17
  109.8 4.6 %collective-permute-start.10 = (bf16[512,1024]{1,0:T(8,128)(2,1)S(1)}, bf16[512,1024]{1,0:T(8,128)(2,1)S(1)}, u32[]{:S(2)}, u32[]{:S(2)}) collective-permute-start(bf16[512,1024]{1,0:T(8,128)(2,1)S(1)} %convolution_convert_fusion), channel_id=1, source_target_pairs={{0,1},{1,0},{2,3},{3,2},{4,5},{5,4},{6,7},{7,6},{8,9},{9,8},{10,11... | collective-permute-start | bytes 3145736 | tf_op jit(solution)/shard_map/ppermute | solution.py:25
  135.5 39.9 %all-to-all-start.4 = ((bf16[16,32,1024]{2,1,0:T(8,128)(2,1)}), bf16[16,32,1024]{2,1,0:T(8,128)(2,1)S(1)}, u32[]{:S(2)}, u32[]{:S(2)}) async-start(bf16[16,32,1024]{2,1,0:T(8,128)(2,1)} %bitcast.57), calls=%async_computation.4 | async-start | bytes 2097152 | tf_op jit(solution)/shard_map/all_to_all | solution.py:17
  141.8 3.1 %collective-permute-start.5 = (f32[8,128]{1,0:T(8,128)S(1)}, f32[8,128]{1,0:T(8,128)S(1)}, u32[]{:S(2)}, u32[]{:S(2)}) collective-permute-start(f32[8,128]{1,0:T(8,128)S(1)} %broadcast_in_dim.52), channel_id=1, source_target_pairs={{0,1},{1,0},{2,3},{3,2},{4,5},{5,4},{6,7},{7,6},{8,9},{9,8},{10,11... | collective-permute-start | bytes 12296 | tf_op jit(solution)/shard_map/ppermute | solution.py:51
  144.8 5.5 %collective-permute-start.6 = (f32[8,128]{1,0:T(8,128)S(1)}, f32[8,128]{1,0:T(8,128)S(1)}, u32[]{:S(2)}, u32[]{:S(2)}) collective-permute-start(f32[8,128]{1,0:T(8,128)S(1)} %broadcast_add_fusion), channel_id=1, source_target_pairs={{0,32},{32,0},{64,96},{96,64},{1,33},{33,1},{65,97},{97,65},{2,34}... | collective-permute-start | bytes 12296 | tf_op jit(solution)/shard_map/ppermute | solution.py:51
  150.3 7.0 %collective-permute-start.7 = (f32[8,128]{1,0:T(8,128)S(1)}, f32[8,128]{1,0:T(8,128)S(1)}, u32[]{:S(2)}, u32[]{:S(2)}) collective-permute-start(f32[8,128]{1,0:T(8,128)S(1)} %fusion.25), channel_id=1, source_target_pairs={{0,64},{32,96},{64,0},{96,32},{1,65},{33,97},{65,1},{97,33},{2,66}... | collective-permute-start | bytes 12296 | tf_op jit(solution)/shard_map/ppermute | solution.py:51
  157.3 6.4 %collective-permute-start.8 = (f32[8,128]{1,0:T(8,128)S(1)}, f32[8,128]{1,0:T(8,128)S(1)}, u32[]{:S(2)}, u32[]{:S(2)}) collective-permute-start(f32[8,128]{1,0:T(8,128)S(1)} %add.112), channel_id=1, source_target_pairs={{0,128},{128,0},{256,384},{384,256},{1,129},{129,1},{257,385},{385... | collective-permute-start | bytes 12296 | tf_op jit(solution)/shard_map/ppermute | solution.py:51
  163.7 9.4 %collective-permute-start.9 = (f32[8,128]{1,0:T(8,128)S(1)}, f32[8,128]{1,0:T(8,128)S(1)}, u32[]{:S(2)}, u32[]{:S(2)}) collective-permute-start(f32[8,128]{1,0:T(8,128)S(1)} %add.113), channel_id=1, source_target_pairs={{0,256},{128,384},{256,0},{384,128},{1,257},{129,385},{257,1},{385... | collective-permute-start | bytes 12296 | tf_op jit(solution)/shard_map/ppermute | solution.py:51

commit v2 on v1

--- a/solution.py
+++ b/solution.py
@@ -64,8 +64,9 @@
     near = exchange(spread(passage, n_yh), "yh").reshape(n_yh * rows, embed)
     own = exchange(spread(query, n_chip), CHIP_AXES).reshape(half, embed)
     far = [shift_x(near, n_x - d) for d in range(1, n_x)]
-    ring = jnp.stack([near] + far + [near] + far[:-1])
-    pall = lax.dynamic_slice_in_dim(ring, (n_x - x_at) % n_x, n_x, 0)
+    pall = jnp.zeros((n_x, n_yh * rows, embed), query.dtype)
+    for d, block in enumerate([near] + far):
+        pall = lax.dynamic_update_slice_in_dim(pall, block[None], (x_at + d) % n_x, 0)
     pall = lax.optimization_barrier(pall.reshape(n_p, embed))
     other = swap_core(own)
 

time: 178 us -> 177 us (level)
  local copies, waits for them, and re-layouts: 11.8 us -> 6.94 us
  waiting for transfers between devices: 69.8 us -> 72.8 us
    all_to_all x5, waiting for transfers between devices: 42 us -> 47.7 us  [exchange(): return lax.all_to_all(blocks, axes, 0, 0, tiled=True)]
    ppermute x3, waiting for transfers between devices: 5.64 us -> 0.01 us  [shift_x(): return lax.ppermute(x, 'x', [(i, (i + d) % n) for i in range(n)])]
    unnamed x20, local copies, waits for them, and re-layouts: 4.51 us -> 1.4 us
    all_to_all x5, starting transfers between devices: 34 us -> 36.5 us  [exchange(): return lax.all_to_all(blocks, axes, 0, 0, tiled=True)]
  transfers between devices with their start and end apart: 16 -> 16, of which waited for: 11 -> 11; matrix products, arithmetic and copies ran while one was open for 10% -> 7% of each run, Pallas kernels for 0% -> 0%
where the time goes in v2:
time: 177 us; the launch traced here: 176 us
  waiting for transfers between devices  72.8 us (41%)
  starting transfers between devices  63.5 us (36%)
  blocking collectives  12.6 us (7%)
  matrix products  10.9 us (6%)
  local copies, waits for them, and re-layouts  6.94 us (4%)
  between operations  5.41 us (3%)
  other arithmetic  3.79 us (2%)
    all_to_all x5, waiting for transfers between devices, exchange(): return lax.all_to_all(blocks, axes, 0, 0, tiled=True)  47.7 us
    all_to_all x5, starting transfers between devices, exchange(): return lax.all_to_all(blocks, axes, 0, 0, tiled=True)  36.5 us
    ppermute x5, waiting for transfers between devices, add_partner(): return x + lax.ppermute(x, axis, [(i, i ^ step) for i in range(n)])  20.9 us
    all_to_all x1, blocking collectives, exchange(): return lax.all_to_all(blocks, axes, 0, 0, tiled=True)  12.6 us
    ppermute x3, starting transfers between devices, shift_x(): return lax.ppermute(x, 'x', [(i, (i + d) % n) for i in range(n)])  10.8 us
    ppermute x5, starting transfers between devices, add_partner(): return x + lax.ppermute(x, axis, [(i, i ^ step) for i in range(n)])  10.3 us
    ppermute x3, starting transfers between devices, swap_core(): return lax.ppermute(x, 'core', [(0, 1), (1, 0)])  5.88 us
    broadcast_in_dim x4, local copies, waits for them, and re-layouts, spread(): return lax.optimization_barrier(jnp.broadcast_to(x[None], (n,) + x.shape))  4.21 us
  transfers between devices with their start and end apart: 16, of which 11 were waited for; matrix products, arithmetic and copies ran while one was open for 7% of the time, Pallas kernels for 0%

profile of v2, /device:TPU:8, one launch (start us, length us, event | category | flops | bytes accessed | tf_op | source)
XLA Modules:
  0.0 175.9 jit_solution(11374909368333369148)
XLA Ops:
  0.7 1.6 broadcast_in_dim.31
  2.3 6.2 %all-to-all-start = ((bf16[4,32,1024]{2,1,0:T(8,128)(2,1)}), bf16[4,32,1024]{2,1,0:T(8,128)(2,1)S(1)}, u32[]{:S(2)}, u32[]{:S(2)}) async-start(bf16[4,32,1024]{2,1,0:T(8,128)(2,1)} %broadcast_in_dim.31), calls=%async_computation | async-start | bytes 524288 | tf_op jit(solution)/shard_map/all_to_all | solution.py:17
  8.5 2.0 %broadcast_in_dim.62 = bf16[16,32,1024]{2,1,0:T(8,128)(2,1)} broadcast(bf16[32,1024]{1,0:T(8,128)(2,1)} %param.3), dimensions={1,2} | broadcast | bytes 1114112 | tf_op jit(solution)/shard_map/broadcast_in_dim | solution.py:21
  10.4 8.0 %all-to-all-done = bf16[4,32,1024]{2,1,0:T(8,128)(2,1)S(1)} async-done(((bf16[4,32,1024]{2,1,0:T(8,128)(2,1)}), bf16[4,32,1024]{2,1,0:T(8,128)(2,1)S(1)}, u32[]{:S(2)}, u32[]{:S(2)}) %all-to-all-start) | async-done | bytes 262176 | tf_op jit(solution)/shard_map/all_to_all | solution.py:17
  18.4 12.1 %all-to-all-start.1 = ((bf16[16,32,1024]{2,1,0:T(8,128)(2,1)}), bf16[16,32,1024]{2,1,0:T(8,128)(2,1)S(1)}, u32[]{:S(2)}, u32[]{:S(2)}) async-start(bf16[16,32,1024]{2,1,0:T(8,128)(2,1)} %broadcast_in_dim.62), calls=%async_computation.1 | async-start | bytes 2097152 | tf_op jit(solution)/shard_map/all_to_all | solution.py:17
  30.5 4.7 %collective-permute-start = (bf16[128,1024]{1,0:T(8,128)(2,1)S(1)}, bf16[128,1024]{1,0:T(8,128)(2,1)S(1)}, u32[]{:S(2)}, u32[]{:S(2)}) collective-permute-start(bf16[128,1024]{1,0:T(8,128)(2,1)S(1)} %bitcast.41), channel_id=1, source_target_pairs={{0,96},{32,0},{64,32},{96,64},{1,97},{33,1},{65,33},{97,65},{2,98}... | collective-permute-start | bytes 786440 | tf_op jit(solution)/shard_map/ppermute | solution.py:30
  35.2 1.5 multiply_reduce_fusion
  37.4 1.9 %collective-permute-start.2 = (bf16[128,1024]{1,0:T(8,128)(2,1)S(1)}, bf16[128,1024]{1,0:T(8,128)(2,1)S(1)}, u32[]{:S(2)}, u32[]{:S(2)}) collective-permute-start(bf16[128,1024]{1,0:T(8,128)(2,1)S(1)} %bitcast.42), channel_id=1, source_target_pairs={{0,32},{32,64},{64,96},{96,0},{1,33},{33,65},{65,97},{97,1},{2,34}... | collective-permute-start | bytes 786440 | tf_op jit(solution)/shard_map/ppermute | solution.py:30
  39.3 4.2 %collective-permute-start.1 = (bf16[128,1024]{1,0:T(8,128)(2,1)S(1)}, bf16[128,1024]{1,0:T(8,128)(2,1)S(1)}, u32[]{:S(2)}, u32[]{:S(2)}) collective-permute-start(bf16[128,1024]{1,0:T(8,128)(2,1)S(1)} %bitcast.43), channel_id=1, source_target_pairs={{0,64},{32,96},{64,0},{96,32},{1,65},{33,97},{65,1},{97,33},{2,66}... | collective-permute-start | bytes 786440 | tf_op jit(solution)/shard_map/ppermute | solution.py:30
  43.5 11.9 %all-to-all-done.1 = bf16[16,32,1024]{2,1,0:T(8,128)(2,1)S(1)} async-done(((bf16[16,32,1024]{2,1,0:T(8,128)(2,1)}), bf16[16,32,1024]{2,1,0:T(8,128)(2,1)S(1)}, u32[]{:S(2)}, u32[]{:S(2)}) %all-to-all-start.1) | async-done | bytes 1048608 | tf_op jit(solution)/shard_map/all_to_all | solution.py:17
  55.4 1.9 %collective-permute-start.3 = (bf16[512,1024]{1,0:T(8,128)(2,1)S(1)}, bf16[512,1024]{1,0:T(8,128)(2,1)S(1)}, u32[]{:S(2)}, u32[]{:S(2)}) collective-permute-start(bf16[512,1024]{1,0:T(8,128)(2,1)S(1)} %bitcast.45), channel_id=1, source_target_pairs={{0,1},{1,0},{2,3},{3,2},{4,5},{5,4},{6,7},{7,6},{8,9},{9,8},{10,11... | collective-permute-start | bytes 3145736 | tf_op jit(solution)/shard_map/ppermute | solution.py:25
  57.6 0.8 fusion.9
  58.5 1.5 collective-permute-done.3
  60.0 1.0 copy-done.8
  61.0 0.8 fusion.10
  61.8 0.7 exponential_reduce_fusion.2
  62.5 2.0 %collective-permute-start.4 = (f32[8,128]{1,0:T(8,128)S(1)}, f32[8,128]{1,0:T(8,128)S(1)}, u32[]{:S(2)}, u32[]{:S(2)}) collective-permute-start(f32[8,128]{1,0:T(8,128)S(1)} %pad_maximum_fusion.1), channel_id=1, source_target_pairs={{0,1},{1,0},{2,3},{3,2},{4,5},{5,4},{6,7},{7,6},{8,9},{9,8},{10,11... | collective-permute-start | bytes 12296 | tf_op jit(solution)/shard_map/ppermute | solution.py:25
  64.6 0.6 broadcast_in_dim.63
  65.2 8.3 %all-to-all-start.2 = ((f32[16,4,128]{2,1,0:T(4,128)}), f32[16,4,128]{2,1,0:T(4,128)S(1)}, u32[]{:S(2)}, u32[]{:S(2)}) async-start(f32[16,4,128]{2,1,0:T(4,128)} %broadcast_in_dim.63), calls=%async_computation.2 | async-start | bytes 65536 | tf_op jit(solution)/shard_map/all_to_all | solution.py:17
  73.5 10.0 %all-to-all-done.2 = f32[16,4,128]{2,1,0:T(4,128)S(1)} async-done(((f32[16,4,128]{2,1,0:T(4,128)}), f32[16,4,128]{2,1,0:T(4,128)S(1)}, u32[]{:S(2)}, u32[]{:S(2)}) %all-to-all-start.2) | async-done | bytes 32800 | tf_op jit(solution)/shard_map/all_to_all | solution.py:17
  83.6 0.6 fusion.6
  84.2 0.6 broadcast_select_fusion
  84.9 12.6 %all_to_all.30 = f32[16,16,128]{2,1,0:T(8,128)S(1)} all-to-all(f32[16,16,128]{2,1,0:T(8,128)S(1)} %broadcast_in_dim.67), channel_id=1, replica_groups=mesh['yh'=4,'x'=4,'z'=8,'yl'=2,'core'=2] {'z','yl'}, dimensions={0} | all-to-all | bytes 262144 | tf_op jit(solution)/shard_map/all_to_all | solution.py:17
  97.5 0.6 fusion.11
  98.1 0.8 fusion.8
  98.9 0.4 copy-done.9
  99.3 1.9 %add_convert_fusion = bf16[512,1024]{1,0:T(8,128)(2,1)} fusion(f32[512,1024]{1,0:T(8,128)S(1)} %fusion.8, bf16[512,1024]{1,0:T(8,128)(2,1)S(1)} %copy-done.9, f32[512,512]{1,0:T(8,128)S(1)} %get-tuple-element.26, f32[512]{0:T(512)S(1)} %get-tuple-element.14, f32[512]{0:T(512)S(1)} %get-tuple-element.15), kind=kOutput, calls=%fused_computation.1 | convolution fusion | flops 539230208 | bytes 5246976 | tf_op jit(solution)/shard_map/dot_general | solution.py:112
  101.2 3.7 %all-to-all-start.5 = ((bf16[16,32,1024]{2,1,0:T(8,128)(2,1)}), bf16[16,32,1024]{2,1,0:T(8,128)(2,1)S(1)}, u32[]{:S(2)}, u32[]{:S(2)}) async-start(bf16[16,32,1024]{2,1,0:T(8,128)(2,1)} %bitcast.48), calls=%async_computation.5 | async-start | bytes 2097152 | tf_op jit(solution)/shard_map/all_to_all | solution.py:17
  104.9 2.2 %convolution_convert_fusion = bf16[512,1024]{1,0:T(8,128)(2,1)S(1)} fusion(bf16[512,1024]{1,0:T(8,128)(2,1)} %bitcast.51, f32[512,512]{1,0:T(8,128)S(1)} %get-tuple-element.26, f32[512]{0:T(512)S(1)} %get-tuple-element.14, f32[512]{0:T(512)S(1)} %get-tuple-element.15), kind=kOutput, calls=%fused_computation.4 | convolution fusion | flops 538705920 | bytes 3149824 | tf_op jit(solution)/shard_map/dot_general | solution.py:116
  107.1 1.9 %collective-permute-start.10 = (bf16[512,1024]{1,0:T(8,128)(2,1)S(1)}, bf16[512,1024]{1,0:T(8,128)(2,1)S(1)}, u32[]{:S(2)}, u32[]{:S(2)}) collective-permute-start(bf16[512,1024]{1,0:T(8,128)(2,1)S(1)} %convolution_convert_fusion), channel_id=1, source_target_pairs={{0,1},{1,0},{2,3},{3,2},{4,5},{5,4},{6,7},{7,6},{8,9},{9,8},{10,11... | collective-permute-start | bytes 3145736 | tf_op jit(solution)/shard_map/ppermute | solution.py:25
  109.0 2.6 %collective-permute-done.10 = bf16[512,1024]{1,0:T(8,128)(2,1)S(1)} collective-permute-done((bf16[512,1024]{1,0:T(8,128)(2,1)S(1)}, bf16[512,1024]{1,0:T(8,128)(2,1)S(1)}, u32[]{:S(2)}, u32[]{:S(2)}) %collective-permute-start.10) | collective-permute-done | bytes 1048608 | tf_op jit(solution)/shard_map/ppermute | solution.py:25
  111.6 1.9 %add_convert_fusion.1 = bf16[512,1024]{1,0:T(8,128)(2,1)} fusion(bf16[512,1024]{1,0:T(8,128)(2,1)S(1)} %collective-permute-done.10, bf16[512,1024]{1,0:T(8,128)(2,1)S(1)} %bitcast.52, f32[512,512]{1,0:T(8,128)S(1)} %get-tuple-element.25, f32[512]{0:T(512)S(1)} %get-tuple-element.15, f32[512]{0:T(512)S(1)} %get-tuple-element.13), kind=kOutput, calls=%fused_computation.3 | convolution fusion | flops 539754496 | bytes 4198400 | tf_op jit(solution)/shard_map/dot_general | solution.py:118
  113.6 17.8 %all-to-all-done.5 = bf16[16,32,1024]{2,1,0:T(8,128)(2,1)S(1)} async-done(((bf16[16,32,1024]{2,1,0:T(8,128)(2,1)}), bf16[16,32,1024]{2,1,0:T(8,128)(2,1)S(1)}, u32[]{:S(2)}, u32[]{:S(2)}) %all-to-all-start.5) | async-done | bytes 1048608 | tf_op jit(solution)/shard_map/all_to_all | solution.py:17
  131.4 6.3 %all-to-all-start.4 = ((bf16[16,32,1024]{2,1,0:T(8,128)(2,1)}), bf16[16,32,1024]{2,1,0:T(8,128)(2,1)S(1)}, u32[]{:S(2)}, u32[]{:S(2)}) async-start(bf16[16,32,1024]{2,1,0:T(8,128)(2,1)} %bitcast.18), calls=%async_computation.4 | async-start | bytes 2097152 | tf_op jit(solution)/shard_map/all_to_all | solution.py:17
  138.4 0.6 fusion.13
  140.3 1.9 %collective-permute-start.5 = (f32[8,128]{1,0:T(8,128)S(1)}, f32[8,128]{1,0:T(8,128)S(1)}, u32[]{:S(2)}, u32[]{:S(2)}) collective-permute-start(f32[8,128]{1,0:T(8,128)S(1)} %broadcast_in_dim.68), channel_id=1, source_target_pairs={{0,1},{1,0},{2,3},{3,2},{4,5},{5,4},{6,7},{7,6},{8,9},{9,8},{10,11... | collective-permute-start | bytes 12296 | tf_op jit(solution)/shard_map/ppermute | solution.py:51
  142.2 1.1 collective-permute-done.5
  143.3 1.9 %collective-permute-start.6 = (f32[8,128]{1,0:T(8,128)S(1)}, f32[8,128]{1,0:T(8,128)S(1)}, u32[]{:S(2)}, u32[]{:S(2)}) collective-permute-start(f32[8,128]{1,0:T(8,128)S(1)} %broadcast_add_fusion), channel_id=1, source_target_pairs={{0,32},{32,0},{64,96},{96,64},{1,33},{33,1},{65,97},{97,65},{2,34}... | collective-permute-start | bytes 12296 | tf_op jit(solution)/shard_map/ppermute | solution.py:51
  145.3 3.6 %collective-permute-done.6 = f32[8,128]{1,0:T(8,128)S(1)} collective-permute-done((f32[8,128]{1,0:T(8,128)S(1)}, f32[8,128]{1,0:T(8,128)S(1)}, u32[]{:S(2)}, u32[]{:S(2)}) %collective-permute-start.6) | collective-permute-done | bytes 4128 | tf_op jit(solution)/shard_map/ppermute | solution.py:51
  148.8 2.7 %collective-permute-start.7 = (f32[8,128]{1,0:T(8,128)S(1)}, f32[8,128]{1,0:T(8,128)S(1)}, u32[]{:S(2)}, u32[]{:S(2)}) collective-permute-start(f32[8,128]{1,0:T(8,128)S(1)} %fusion.24), channel_id=1, source_target_pairs={{0,64},{32,96},{64,0},{96,32},{1,65},{33,97},{65,1},{97,33},{2,66}... | collective-permute-start | bytes 12296 | tf_op jit(solution)/shard_map/ppermute | solution.py:51
  151.6 4.3 %collective-permute-done.7 = f32[8,128]{1,0:T(8,128)S(1)} collective-permute-done((f32[8,128]{1,0:T(8,128)S(1)}, f32[8,128]{1,0:T(8,128)S(1)}, u32[]{:S(2)}, u32[]{:S(2)}) %collective-permute-start.7) | collective-permute-done | bytes 4128 | tf_op jit(solution)/shard_map/ppermute | solution.py:51
  155.8 1.9 %collective-permute-start.8 = (f32[8,128]{1,0:T(8,128)S(1)}, f32[8,128]{1,0:T(8,128)S(1)}, u32[]{:S(2)}, u32[]{:S(2)}) collective-permute-start(f32[8,128]{1,0:T(8,128)S(1)} %add.148), channel_id=1, source_target_pairs={{0,128},{128,0},{256,384},{384,256},{1,129},{129,1},{257,385},{385... | collective-permute-start | bytes 12296 | tf_op jit(solution)/shard_map/ppermute | solution.py:51
  157.8 4.5 %collective-permute-done.8 = f32[8,128]{1,0:T(8,128)S(1)} collective-permute-done((f32[8,128]{1,0:T(8,128)S(1)}, f32[8,128]{1,0:T(8,128)S(1)}, u32[]{:S(2)}, u32[]{:S(2)}) %collective-permute-start.8) | collective-permute-done | bytes 4128 | tf_op jit(solution)/shard_map/ppermute | solution.py:51
  162.2 1.9 %collective-permute-start.9 = (f32[8,128]{1,0:T(8,128)S(1)}, f32[8,128]{1,0:T(8,128)S(1)}, u32[]{:S(2)}, u32[]{:S(2)}) collective-permute-start(f32[8,128]{1,0:T(8,128)S(1)} %add.149), channel_id=1, source_target_pairs={{0,256},{128,384},{256,0},{384,128},{1,257},{129,385},{257,1},{385... | collective-permute-start | bytes 12296 | tf_op jit(solution)/shard_map/ppermute | solution.py:51
  164.2 7.5 %collective-permute-done.9 = f32[8,128]{1,0:T(8,128)S(1)} collective-permute-done((f32[8,128]{1,0:T(8,128)S(1)}, f32[8,128]{1,0:T(8,128)S(1)}, u32[]{:S(2)}, u32[]{:S(2)}) %collective-permute-start.9) | collective-permute-done | bytes 4128 | tf_op jit(solution)/shard_map/ppermute | solution.py:51
  171.6 0.5 slice.33
  173.0 0.9 fusion.1
  174.1 0.6 multiply_convert_fusion.2
  (53 shorter events, 0.9 us)
Async XLA Ops:
  0.6 34.6 %copy-start.6 = (bf16[32,1024]{1,0:T(8,128)(2,1)S(1)}, bf16[32,1024]{1,0:T(8,128)(2,1)}, u32[]{:S(2)}) copy-start(bf16[32,1024]{1,0:T(8,128)(2,1)} %param.4) | copy-start | bytes 196612
  0.6 34.6 %copy-start.4 = (bf16[32,1024]{1,0:T(8,128)(2,1)S(1)}, bf16[32,1024]{1,0:T(8,128)(2,1)}, u32[]{:S(2)}) copy-start(bf16[32,1024]{1,0:T(8,128)(2,1)} %param.3) | copy-start | bytes 196612
  0.7 34.6 %copy-start.7 = (s32[1,32]{1,0:T(1,128)S(1)}, s32[1,32]{1,0:T(1,128)}, u32[]{:S(2)}) copy-start(s32[1,32]{1,0:T(1,128)} %param.5) | copy-start | bytes 388
  2.3 16.1 %all-to-all-start = ((bf16[4,32,1024]{2,1,0:T(8,128)(2,1)}), bf16[4,32,1024]{2,1,0:T(8,128)(2,1)S(1)}, u32[]{:S(2)}, u32[]{:S(2)}) async-start(bf16[4,32,1024]{2,1,0:T(8,128)(2,1)} %broadcast_in_dim.31), calls=%async_computation | async-start | bytes 524288 | tf_op jit(solution)/shard_map/all_to_all | solution.py:17
  18.4 37.0 %all-to-all-start.1 = ((bf16[16,32,1024]{2,1,0:T(8,128)(2,1)}), bf16[16,32,1024]{2,1,0:T(8,128)(2,1)S(1)}, u32[]{:S(2)}, u32[]{:S(2)}) async-start(bf16[16,32,1024]{2,1,0:T(8,128)(2,1)} %broadcast_in_dim.62), calls=%async_computation.1 | async-start | bytes 2097152 | tf_op jit(solution)/shard_map/all_to_all | solution.py:17
  30.5 27.0 %collective-permute-start = (bf16[128,1024]{1,0:T(8,128)(2,1)S(1)}, bf16[128,1024]{1,0:T(8,128)(2,1)S(1)}, u32[]{:S(2)}, u32[]{:S(2)}) collective-permute-start(bf16[128,1024]{1,0:T(8,128)(2,1)S(1)} %bitcast.41), channel_id=1, source_target_pairs={{0,96},{32,0},{64,32},{96,64},{1,97},{33,1},{65,33},{97,65},{2,98}... | collective-permute-start | bytes 786440 | tf_op jit(solution)/shard_map/ppermute | solution.py:30
  37.4 20.2 %collective-permute-start.2 = (bf16[128,1024]{1,0:T(8,128)(2,1)S(1)}, bf16[128,1024]{1,0:T(8,128)(2,1)S(1)}, u32[]{:S(2)}, u32[]{:S(2)}) collective-permute-start(bf16[128,1024]{1,0:T(8,128)(2,1)S(1)} %bitcast.42), channel_id=1, source_target_pairs={{0,32},{32,64},{64,96},{96,0},{1,33},{33,65},{65,97},{97,1},{2,34}... | collective-permute-start | bytes 786440 | tf_op jit(solution)/shard_map/ppermute | solution.py:30
  39.3 18.3 %collective-permute-start.1 = (bf16[128,1024]{1,0:T(8,128)(2,1)S(1)}, bf16[128,1024]{1,0:T(8,128)(2,1)S(1)}, u32[]{:S(2)}, u32[]{:S(2)}) collective-permute-start(bf16[128,1024]{1,0:T(8,128)(2,1)S(1)} %bitcast.43), channel_id=1, source_target_pairs={{0,64},{32,96},{64,0},{96,32},{1,65},{33,97},{65,1},{97,33},{2,66}... | collective-permute-start | bytes 786440 | tf_op jit(solution)/shard_map/ppermute | solution.py:30
  55.4 3.0 %copy-start = (bf16[16,32,1024]{2,1,0:T(8,128)(2,1)}, bf16[16,32,1024]{2,1,0:T(8,128)(2,1)S(1)}, u32[]{:S(2)}) copy-start(bf16[16,32,1024]{2,1,0:T(8,128)(2,1)S(1)} %all-to-all-done.1) | copy-start | bytes 3145732
  55.4 4.5 %collective-permute-start.3 = (bf16[512,1024]{1,0:T(8,128)(2,1)S(1)}, bf16[512,1024]{1,0:T(8,128)(2,1)S(1)}, u32[]{:S(2)}, u32[]{:S(2)}) collective-permute-start(bf16[512,1024]{1,0:T(8,128)(2,1)S(1)} %bitcast.45), channel_id=1, source_target_pairs={{0,1},{1,0},{2,3},{3,2},{4,5},{5,4},{6,7},{7,6},{8,9},{9,8},{10,11... | collective-permute-start | bytes 3145736 | tf_op jit(solution)/shard_map/ppermute | solution.py:25
  57.6 4.2 %copy-start.2 = (bf16[4,128,1024]{2,1,0:T(8,128)(2,1)}, bf16[4,128,1024]{2,1,0:T(8,128)(2,1)S(1)}, u32[]{:S(2)}) copy-start(bf16[4,128,1024]{2,1,0:T(8,128)(2,1)S(1)} %bitcast_dynamic-update-slice_fusion) | copy-start | bytes 3145732
  60.0 1.0 copy-start.8
  61.8 36.3 %copy-start.1 = (bf16[16,32,1024]{2,1,0:T(8,128)(2,1)S(1)}, bf16[16,32,1024]{2,1,0:T(8,128)(2,1)}, u32[]{:S(2)}) copy-start(bf16[16,32,1024]{2,1,0:T(8,128)(2,1)} %copy-done) | copy-start | bytes 3145732
  62.5 11.0 %collective-permute-start.4 = (f32[8,128]{1,0:T(8,128)S(1)}, f32[8,128]{1,0:T(8,128)S(1)}, u32[]{:S(2)}, u32[]{:S(2)}) collective-permute-start(f32[8,128]{1,0:T(8,128)S(1)} %pad_maximum_fusion.1), channel_id=1, source_target_pairs={{0,1},{1,0},{2,3},{3,2},{4,5},{5,4},{6,7},{7,6},{8,9},{9,8},{10,11... | collective-permute-start | bytes 12296 | tf_op jit(solution)/shard_map/ppermute | solution.py:25
  65.2 18.3 %all-to-all-start.2 = ((f32[16,4,128]{2,1,0:T(4,128)}), f32[16,4,128]{2,1,0:T(4,128)S(1)}, u32[]{:S(2)}, u32[]{:S(2)}) async-start(f32[16,4,128]{2,1,0:T(4,128)} %broadcast_in_dim.63), calls=%async_computation.2 | async-start | bytes 65536 | tf_op jit(solution)/shard_map/all_to_all | solution.py:17
  98.1 1.2 copy-start.9
  101.2 30.2 %all-to-all-start.5 = ((bf16[16,32,1024]{2,1,0:T(8,128)(2,1)}), bf16[16,32,1024]{2,1,0:T(8,128)(2,1)S(1)}, u32[]{:S(2)}, u32[]{:S(2)}) async-start(bf16[16,32,1024]{2,1,0:T(8,128)(2,1)} %bitcast.48), calls=%async_computation.5 | async-start | bytes 2097152 | tf_op jit(solution)/shard_map/all_to_all | solution.py:17
  104.9 6.8 %copy-start.3 = (bf16[4,128,1024]{2,1,0:T(8,128)(2,1)S(1)}, bf16[4,128,1024]{2,1,0:T(8,128)(2,1)}, u32[]{:S(2)}) copy-start(bf16[4,128,1024]{2,1,0:T(8,128)(2,1)} %copy-done.2) | copy-start | bytes 3145732
  107.1 4.6 %collective-permute-start.10 = (bf16[512,1024]{1,0:T(8,128)(2,1)S(1)}, bf16[512,1024]{1,0:T(8,128)(2,1)S(1)}, u32[]{:S(2)}, u32[]{:S(2)}) collective-permute-start(bf16[512,1024]{1,0:T(8,128)(2,1)S(1)} %convolution_convert_fusion), channel_id=1, source_target_pairs={{0,1},{1,0},{2,3},{3,2},{4,5},{5,4},{6,7},{7,6},{8,9},{9,8},{10,11... | collective-permute-start | bytes 3145736 | tf_op jit(solution)/shard_map/ppermute | solution.py:25
  131.4 42.7 %copy-start.5 = (f32[32,1024]{1,0:T(8,128)S(1)}, f32[32,1024]{1,0:T(8,128)}, u32[]{:S(2)}) copy-start(f32[32,1024]{1,0:T(8,128)} %get-tuple-element.24) | copy-start | bytes 393220
  131.4 42.5 %all-to-all-start.4 = ((bf16[16,32,1024]{2,1,0:T(8,128)(2,1)}), bf16[16,32,1024]{2,1,0:T(8,128)(2,1)S(1)}, u32[]{:S(2)}, u32[]{:S(2)}) async-start(bf16[16,32,1024]{2,1,0:T(8,128)(2,1)} %bitcast.18), calls=%async_computation.4 | async-start | bytes 2097152 | tf_op jit(solution)/shard_map/all_to_all | solution.py:17
  140.3 3.1 %collective-permute-start.5 = (f32[8,128]{1,0:T(8,128)S(1)}, f32[8,128]{1,0:T(8,128)S(1)}, u32[]{:S(2)}, u32[]{:S(2)}) collective-permute-start(f32[8,128]{1,0:T(8,128)S(1)} %broadcast_in_dim.68), channel_id=1, source_target_pairs={{0,1},{1,0},{2,3},{3,2},{4,5},{5,4},{6,7},{7,6},{8,9},{9,8},{10,11... | collective-permute-start | bytes 12296 | tf_op jit(solution)/shard_map/ppermute | solution.py:51
  143.3 5.5 %collective-permute-start.6 = (f32[8,128]{1,0:T(8,128)S(1)}, f32[8,128]{1,0:T(8,128)S(1)}, u32[]{:S(2)}, u32[]{:S(2)}) collective-permute-start(f32[8,128]{1,0:T(8,128)S(1)} %broadcast_add_fusion), channel_id=1, source_target_pairs={{0,32},{32,0},{64,96},{96,64},{1,33},{33,1},{65,97},{97,65},{2,34}... | collective-permute-start | bytes 12296 | tf_op jit(solution)/shard_map/ppermute | solution.py:51
  148.8 7.0 %collective-permute-start.7 = (f32[8,128]{1,0:T(8,128)S(1)}, f32[8,128]{1,0:T(8,128)S(1)}, u32[]{:S(2)}, u32[]{:S(2)}) collective-permute-start(f32[8,128]{1,0:T(8,128)S(1)} %fusion.24), channel_id=1, source_target_pairs={{0,64},{32,96},{64,0},{96,32},{1,65},{33,97},{65,1},{97,33},{2,66}... | collective-permute-start | bytes 12296 | tf_op jit(solution)/shard_map/ppermute | solution.py:51
  155.8 6.4 %collective-permute-start.8 = (f32[8,128]{1,0:T(8,128)S(1)}, f32[8,128]{1,0:T(8,128)S(1)}, u32[]{:S(2)}, u32[]{:S(2)}) collective-permute-start(f32[8,128]{1,0:T(8,128)S(1)} %add.148), channel_id=1, source_target_pairs={{0,128},{128,0},{256,384},{384,256},{1,129},{129,1},{257,385},{385... | collective-permute-start | bytes 12296 | tf_op jit(solution)/shard_map/ppermute | solution.py:51
  162.2 9.4 %collective-permute-start.9 = (f32[8,128]{1,0:T(8,128)S(1)}, f32[8,128]{1,0:T(8,128)S(1)}, u32[]{:S(2)}, u32[]{:S(2)}) collective-permute-start(f32[8,128]{1,0:T(8,128)S(1)} %add.149), channel_id=1, source_target_pairs={{0,256},{128,384},{256,0},{384,128},{1,257},{129,385},{257,1},{385... | collective-permute-start | bytes 12296 | tf_op jit(solution)/shard_map/ppermute | solution.py:51
